TPU v7x, 512 devices: a whole 4x8x8 slice. The times are simulated.
512 devices in a mesh: tm: 128 (over z, y, core), panel: 4 (over x).
Axes of the slice: x: 4, y: 8, z: 8, core: 2. Of those that a mesh axis runs over, the one named last changes fastest.
Arguments:
- transitions: float32 [256, 1024, 1024], P('tm', None, 'panel'), may hold values from 0 to 1, as said below
- start_weights: float32 [1024], replicated, may hold values from 0.1 to 10
Outputs:
- window_kernel: float32 [128, 1024, 1024], P('tm', None, 'panel')
- occupancy: float32 [128, 1024], P('tm', 'panel')
Inputs may be any that keep to these rules, and one draw needn't show every extreme that they name: `transitions`: every entry is nonnegative; each diagonal entry is 0.3 or more; each row sums to between 0.3 and 1.7.
All inputs are finite; a program needn't handle non-finite values.
Results may differ from a plain program's by a relative error of at most 0.0003.
Values sent between devices are 32-bit elements; how exact they have to be, the bound alone decides.
No kernel may reach another device: no remote copies, remote signals or barrier semaphores. Data moves between devices by JAX's collectives and lax.ppermute only.
A program may use at most 64 MiB of HBM per device.

v0:
```python
import jax
import jax.numpy as jnp
from jax import lax
from jax.sharding import PartitionSpec as P

LEVELS = 2


def passed_along(array, axis, by):
    size = lax.axis_size(axis)
    pairs = [(i, i + by) for i in range(size) if 0 <= i + by < size]
    return lax.ppermute(array, axis, pairs)


def matmul_high(left, right):
    return jnp.dot(left, right, precision=lax.Precision.HIGHEST, preferred_element_type=jnp.float32)


def make_adder(right, piece):
    return matmul_high(piece, right)


def body(transitions, start_weights):
    states = transitions.shape[1]
    panel_cols = transitions.shape[2]
    position = lax.axis_index("tm")
    current = transitions[0]
    current = make_adder(transitions[1], lax.all_gather(current, "panel", axis=1, tiled=True))
    whole = lax.all_gather(current, "panel", axis=1, tiled=True)
    column_start = lax.axis_index("panel") * panel_cols
    for level in range(LEVELS):
        reach = 2**level
        earlier = passed_along(whole, "tm", reach)
        if level + 1 < LEVELS:
            joined = matmul_high(earlier, whole)
            whole = jnp.where(position >= reach, joined, whole)
        else:
            mine = lax.dynamic_slice_in_dim(whole, column_start, panel_cols, 1)
            joined = matmul_high(earlier, mine)
            current = jnp.where(position >= reach, joined, mine)
    window_kernel = (current * jnp.float32(states))[None]
    occupancy = matmul_high(start_weights[None, :], current)
    return (window_kernel, occupancy)


def solution(mesh):
    placed = (P("tm", None, "panel"), P())
    return jax.shard_map(
        body,
        mesh=mesh,
        in_specs=placed,
        out_specs=(P("tm", None, "panel"), P("tm", "panel")),
        check_vma=False,
    )
```

profile of v0, /device:TPU:64, one launch (start us, length us, event | category | flops | bytes accessed | tf_op | source)
XLA Modules:
  0.0 308.6 jit_solution(11338718463536803133)
XLA Ops:
  7.2 0.0 copy-start
  7.2 0.0 all-gather.6.cloned.1.call-start
  7.2 2.3 slice.6
  9.5 0.0 all-gather.6.cloned.1.call-update
  9.5 0.0 all-gather.4.cloned.1.call-start
  9.6 58.6 %all-gather.6.cloned.1.call-done = f32[1,1024,1024]{2,1,0:T(8,128)} async-done(((f32[1,1024,256]{2,1,0:T(8,128)}), f32[1,1024,1024]{2,1,0:T(8,128)}) %all-gather.6.cloned.1.call-update) | async-done | bytes 4194320 | tf_op jit(solution)/shard_map/all_gather | solution.py:28
  68.1 6.9 %fusion = f32[1024,256]{1,0:T(8,128)} fusion(f32[1,1024,1024]{2,1,0:T(8,128)} %all-gather.6.cloned.1.call-done, f32[2,1024,256]{2,1,0:T(8,128)} %param.2), kind=kOutput, calls=%fused_computation | convolution fusion | flops 3221225472 | bytes 6291456 | tf_op jit(solution)/shard_map/dot_general | solution.py:16
  75.0 0.0 all-gather.4.cloned.1.call-update
  75.0 54.1 %all-gather.4.cloned.1.call-done = f32[1024,1024]{1,0:T(8,128)} async-done(((f32[1024,256]{1,0:T(8,128)}), f32[1024,1024]{1,0:T(8,128)}) %all-gather.4.cloned.1.call-update) | async-done | bytes 4194320 | tf_op jit(solution)/shard_map/all_gather | solution.py:29
  129.1 1.9 collective-permute-start
  131.0 50.3 %collective-permute-done = f32[1024,1024]{1,0:T(8,128)} collective-permute-done((f32[1024,1024]{1,0:T(8,128)}, f32[1024,1024]{1,0:T(8,128)}, u32[]{:S(2)}, u32[]{:S(2)}) %collective-permute-start) | collective-permute-done | bytes 4194336 | tf_op jit(solution)/shard_map/ppermute | solution.py:12
  181.4 18.2 %convolution_select_fusion = f32[1024,1024]{1,0:T(8,128)} fusion(f32[1024,1024]{1,0:T(8,128)} %all-gather.4.cloned.1.call-done, f32[1024,1024]{1,0:T(8,128)} %collective-permute-done, pred[]{:T(512)S(6)} %ge.7), kind=kOutput, calls=%fused_computation.2 | convolution fusion | flops 12885950464 | bytes 12582913 | tf_op jit(solution)/shard_map/dot_general | solution.py:16
  199.5 2.1 collective-permute-start.1
  201.6 91.7 %collective-permute-done.1 = f32[1024,1024]{1,0:T(8,128)} collective-permute-done((f32[1024,1024]{1,0:T(8,128)}, f32[1024,1024]{1,0:T(8,128)}, u32[]{:S(2)}, u32[]{:S(2)}) %collective-permute-start.1) | collective-permute-done | bytes 4194336 | tf_op jit(solution)/shard_map/ppermute | solution.py:12
  293.3 6.2 %convolution_select_fusion.1 = f32[1024,256]{1,0:T(8,128)S(1)} fusion(f32[1024,1024]{1,0:T(8,128)} %collective-permute-done.1, f32[1024,1024]{1,0:T(8,128)} %convolution_select_fusion, s32[]{:T(128)S(6)} %select_n.22, pred[]{:T(512)S(6)} %ge.6), kind=kOutput, calls=%fused_computation.3 | convolution fusion | flops 3221487616 | bytes 7341568 | tf_op jit(solution)/shard_map/dot_general | solution.py:16
  299.6 1.0 multiply_bitcast_fusion
  300.6 0.0 copy-done
  300.6 1.2 fusion.6
Async XLA Ops:
  7.2 293.5 %copy-start = (f32[1024]{0:T(1024)S(1)}, f32[1024]{0:T(1024)}, u32[]{:S(2)}) copy-start(f32[1024]{0:T(1024)} %param.3) | copy-start | bytes 12292
  7.2 61.0 %all-gather.6.cloned.1.call-start = ((), (), s32[]{:S(2)}) async-start(), calls=%async_computation.1 | async-start | bytes 5242880 | tf_op jit(solution)/shard_map/all_gather | solution.py:28
  9.5 119.6 %all-gather.4.cloned.1.call-start = ((), (), s32[]{:S(2)}) async-start(), calls=%async_computation | async-start | bytes 5242880 | tf_op jit(solution)/shard_map/all_gather | solution.py:29
  129.1 52.2 %collective-permute-start = (f32[1024,1024]{1,0:T(8,128)}, f32[1024,1024]{1,0:T(8,128)}, u32[]{:S(2)}, u32[]{:S(2)}) collective-permute-start(f32[1024,1024]{1,0:T(8,128)} %all-gather.4.cloned.1.call-done), channel_id=1, source_target_pairs={{0,4},{4,8},{8,12},{12,16},{16,20},{20,24},{24,28},{28,32},{32,36}... | collective-permute-start | bytes 12582920 | tf_op jit(solution)/shard_map/ppermute | solution.py:12
  199.5 93.8 %collective-permute-start.1 = (f32[1024,1024]{1,0:T(8,128)}, f32[1024,1024]{1,0:T(8,128)}, u32[]{:S(2)}, u32[]{:S(2)}) collective-permute-start(f32[1024,1024]{1,0:T(8,128)} %convolution_select_fusion), channel_id=1, source_target_pairs={{0,8},{4,12},{8,16},{12,20},{16,24},{20,28},{24,32},{28,36},{32,40... | collective-permute-start | bytes 12582920 | tf_op jit(solution)/shard_map/ppermute | solution.py:12
Sparse Core Ops, SparseCore 0:
  10.7 57.4 all-gather.5
  75.2 53.9 all-gather.3
where the time goes:
time: 309 us
  waiting for transfers between devices  255 us (83%)
  matrix products  32.5 us (11%)
  between operations  14.1 us (5%)
  starting transfers between devices  4.08 us (1%)
    ppermute x2, waiting for transfers between devices, passed_along(): return lax.ppermute(array, axis, pairs)  142 us
    all_gather x1, waiting for transfers between devices, body(): lax.all_gather(current, 'panel', axis=1, tiled=True)  58.6 us
    all_gather x1, waiting for transfers between devices, body(): whole = lax.all_gather(current, 'panel', axis=1, tiled=True)  54.1 us
    dot_general x4, matrix products, matmul_high(): jnp.dot(left, right, precision=lax.Precision.HIGHEST, preferred_element_t...  32.5 us
  transfers between devices with their start and end apart: 4, of which 4 were waited for; matrix products, arithmetic and copies ran while one was open for 0% of the time, Pallas kernels for 0%

commit v1 on v0

v1 whole, which is shorter than its diff:
```python
import functools

import jax
import jax.numpy as jnp
from jax import lax
from jax.experimental import pallas as pl
from jax.experimental.pallas import tpu as pltpu
from jax.sharding import PartitionSpec as P


TILE = 256
CHAIN_TILE = 512


def spec(panel, rows, index):
    a, j = panel
    if j is None:
        return pl.BlockSpec((rows, a.shape[1]), lambda i: (index(i), 0))
    return pl.BlockSpec((None, rows, a.shape[2]), lambda i: (j, index(i), 0))


def place():
    b = lax.axis_index("tm")
    return b // 2, lax.rem(b, 2), lax.axis_index("panel")


def high_low(a):
    high = a.astype(jnp.bfloat16)
    return high, (a - high.astype(jnp.float32)).astype(jnp.bfloat16)


def dot3(high, low, v_high, v_low):
    dot = functools.partial(jnp.dot, preferred_element_type=jnp.float32)
    return dot(high, v_high) + (dot(high, v_low) + dot(low, v_high))


def tile_product(x, left_refs, v_high, v_low):
    total = None
    for r, ref in enumerate(left_refs):
        depth = ref.shape[1]
        rows = pl.ds(pl.multiple_of(lax.rem(x + r, len(left_refs)) * depth, depth), depth)
        part = dot3(*high_low(ref[...]), v_high[rows, :], v_low[rows, :])
        total = part if total is None else total + part
    return total


def put(v_high, v_low, where, value):
    v_high[where], v_low[where] = high_low(value)


def call_kernel(kernel, out_shape, grid, specs, out_specs, scratch, args, flops, traffic):
    return pl.pallas_call(
        kernel,
        out_shape=out_shape,
        grid=(grid,),
        in_specs=specs,
        out_specs=out_specs,
        scratch_shapes=scratch,
        compiler_params=pltpu.CompilerParams(vmem_limit_bytes=67_000_000),
        cost_estimate=pl.CostEstimate(flops=flops, bytes_accessed=traffic, transcendentals=0),
    )(*args)


def only(on, index):
    return lambda i: jnp.where(place()[1] == on, index(i), 0)


def product_kernel(n_left, n_right, width, on, *refs):
    lefts, rights, (out, v_high, v_low) = refs[:n_left], refs[n_left : n_left + n_right], refs[n_left + n_right :]
    i = pl.program_id(0)
    _, core, x = place()

    @pl.when(core == on)
    def _():
        @pl.when(i == 0)
        def _():
            for j, ref in enumerate(rights):
                put(v_high, v_low, (slice(None), slice(j * width, (j + 1) * width)), ref[...])

        total = tile_product(x, lefts, v_high, v_low)
        for j in range(n_right):
            out[j] = total[:, j * width : (j + 1) * width]


def product(left, right, on):
    rows, depth = left[0][0].shape[-2:]
    width = right[0][0].shape[-1]
    n, full = len(right), len(left) * depth
    return call_kernel(
        functools.partial(product_kernel, len(left), n, width, on),
        jax.ShapeDtypeStruct((n, rows, width), jnp.float32),
        rows // TILE,
        [spec(p, TILE, only(on, lambda i: i)) for p in left] + [spec(p, rows, lambda i: 0) for p in right],
        pl.BlockSpec((n, TILE, width), lambda i: (0, only(on, lambda i: i)(i), 0)),
        [pltpu.VMEM((full, n * width), jnp.bfloat16)] * 2,
        [p[0] for p in left + right],
        6 * rows * full * n * width,
        4 * (rows * full + 2 * n * rows * width),
    )


def chain_kernel(counts, tiles, on, passes, *refs):
    n_left = sum(counts)
    lefts, (right, out, v_high, v_low) = refs[:n_left], refs[n_left:]
    i = pl.program_id(0)
    k, core, x = place()
    own = pl.ds(pl.multiple_of(lax.rem(i, tiles) * CHAIN_TILE, CHAIN_TILE), CHAIN_TILE)
    active = core == on

    @pl.when(active & (i == 0))
    def _():
        put(v_high, v_low, 0, right[...])

    at = 0
    for n, count in enumerate(counts):
        here = lefts[at : at + count]
        at += count
        now, later, last = n % 2, (n + 1) % 2, n + 1 == len(counts)

        def keep(total, later=later, last=last):
            if last:
                out[...] = total
            else:
                put(v_high, v_low, (later, own), total)

        mine = active & (i >= n * tiles) & (i < (n + 1) * tiles)
        skipped = passes[n] & (k == 0)

        @pl.when(mine & jnp.logical_not(skipped))
        def _(here=here, now=now, keep=keep):
            keep(tile_product(x, here, v_high.at[now], v_low.at[now]))

        @pl.when(mine & skipped)
        def _(now=now, keep=keep):
            keep(v_high[now, own, :].astype(jnp.float32) + v_low[now, own, :].astype(jnp.float32))


def chain(lefts, right, on, passes):
    rows, _ = lefts[0][0][0].shape[-2:]
    width = right[0].shape[-1]
    tiles, n = rows // CHAIN_TILE, len(lefts)
    specs = []
    for m, left in enumerate(lefts):
        specs += [spec(p, CHAIN_TILE, only(on, lambda i, m=m: jnp.clip(i - m * tiles, 0, tiles - 1))) for p in left]
    return call_kernel(
        functools.partial(chain_kernel, [len(left) for left in lefts], tiles, on, passes),
        jax.ShapeDtypeStruct((rows, width), jnp.float32),
        n * tiles,
        specs + [spec(right, rows, lambda i: 0)],
        pl.BlockSpec((CHAIN_TILE, width), lambda i: (only(on, lambda i: jnp.maximum(i - (n - 1) * tiles, 0))(i), 0)),
        [pltpu.VMEM((2, rows, width), jnp.bfloat16)] * 2,
        [p[0] for left in lefts for p in left] + [right[0]],
        6 * n * rows * rows * width,
        4 * (n * rows * rows + 2 * rows * width),
    )


def finish_kernel(scale, late, whole, early, start, token, window, occupancy):
    i = pl.program_id(0)
    k, core, _ = place()

    def write(ref):
        w = ref[...]
        window[...] = w * scale
        part = dot3(*high_low(start[...]), *high_low(w))
        occupancy[...] = jnp.where(i == 0, part, occupancy[...] + part)

    pl.when(core == 1)(functools.partial(write, late))
    pl.when((core == 0) & (k == 0))(functools.partial(write, whole))
    pl.when((core == 0) & (k > 0))(functools.partial(write, early))


def finish(late, whole, early, start, token):
    rows, width = late.shape
    tiles = [spec(p, CHAIN_TILE, lambda i: i) for p in ((late, None), whole, (early, None))]
    return call_kernel(
        functools.partial(finish_kernel, float(rows)),
        [jax.ShapeDtypeStruct((rows, width), jnp.float32), jax.ShapeDtypeStruct((1, width), jnp.float32)],
        rows // CHAIN_TILE,
        tiles + [pl.BlockSpec((1, CHAIN_TILE), lambda i: (0, i)), pl.BlockSpec(memory_space=pl.ANY)],
        [pl.BlockSpec((CHAIN_TILE, width), lambda i: (i, 0)), pl.BlockSpec((1, width), lambda i: (0, 0))],
        [],
        [late, whole[0], early, start, token],
        4 * rows * width,
        16 * rows * width,
    )


def body(transitions, start_weights):
    n_tm, n_x = lax.axis_size("tm"), lax.axis_size("panel")
    n_chips = n_tm // 2

    def send(a, even=None, odd=None, wrap=False):
        pairs = []
        for kk in range(n_chips):
            for cc, to in enumerate((even, odd)):
                for xx in range(n_x):
                    if to is not None and (wrap or 0 <= kk + to[0] < n_chips):
                        there = (kk + to[0]) % n_chips * 2 + to[1]
                        pairs.append(((kk * 2 + cc) * n_x + xx, there * n_x + (xx + to[2]) % n_x))
        return lax.ppermute(a, ("tm", "panel"), pairs)

    a, c = transitions[0], lax.optimization_barrier(transitions)[1]
    a_left = send(a, (0, 0, 1), (1, 1, 0), wrap=True)
    c_right = send(c, (0, 0, -1))
    c_left = send(c, (0, 0, 1), (1, 1, 0), wrap=True)
    a_right = send(a, (0, 0, -1))
    a_far = send(a_left, (0, 0, 1))
    c_far = send(c_right, (0, 0, -1))
    token = send(c_left[:8, :128], (0, 1, 0))
    a_odd, c_odd = a_left, c_left
    a_odd_left = send(a_odd, None, (0, 1, 1))
    a_odd_right = send(a_odd, None, (0, 1, -1))
    c_odd_right = send(c_odd, None, (0, 1, -1))
    a_odd_far = send(a_odd_left, None, (0, 1, 1))
    c_odd_left = send(c_odd, None, (0, 1, 1))
    c_odd_far = send(c_odd_right, None, (0, 1, -1))

    def panels(own, right, far, left):
        return [own, (right, None), (far, None), (left, None)]

    def stacked(p):
        return [(p, j) for j in range(n_x)]

    left = panels((transitions, 0), a_right, a_far, a_left)
    right = panels((transitions, 1), c_right, c_far, c_left)
    even = product(left, right, 0)
    even_here = stacked(send(even, (0, 1, 0)))
    even_before = stacked(send(even, (1, 1, 0)))
    left = panels((a_odd, None), a_odd_right, a_odd_far, a_odd_left)
    right = panels((c_odd, None), c_odd_right, c_odd_far, c_odd_left)
    step = chain([right, left], even_here[0], 1, (True, True))
    there = send(step, None, (-1, 1, 0))
    ahead = chain([left], right[0], 1, (False,))
    ahead = send(ahead, None, (-1, 0, 0), wrap=True)
    odd = stacked(product(left, right, 1))
    cross = chain([stacked(even)], (ahead, None), 0, (False,))
    cross = send(cross, (0, 1, 0))
    step = chain([even_here, odd], (there, None), 1, (False, True))
    early = send(step, None, (1, 0, 0))
    late = chain([odd, even_before], (cross, None), 1, (True, True))
    window, occupancy = finish(late, (even, 0), early, start_weights[None, :], token)
    return window[None], occupancy


def solution(mesh):
    return jax.shard_map(
        body,
        mesh=mesh,
        in_specs=(P("tm", None, "panel"), P()),
        out_specs=(P("tm", None, "panel"), P("tm", "panel")),
        check_vma=False,
    )
```

time: 309 us -> 146 us (0.47)
  the two profiles are of different devices: /device:TPU:64 before, /device:TPU:14 now
where the time goes in v1:
time: 146 us
  starting transfers between devices  59.1 us (40%)
  waiting for transfers between devices  43.4 us (30%)
  Pallas kernels  36.2 us (25%)
  local copies, waits for them, and re-layouts  6.23 us (4%)
    ppermute x19, starting transfers between devices, send(): return lax.ppermute(a, ('tm', 'panel'), pairs)  59.1 us
    ppermute x19, waiting for transfers between devices, send(): return lax.ppermute(a, ('tm', 'panel'), pairs)  43.4 us
    pallas_call x8, Pallas kernels, call_kernel(): pl.pallas_call(kernel, out_shape=out_shape, grid=(grid,), in_specs=specs,...  36.2 us
    unnamed x12, local copies, waits for them, and re-layouts  2.95 us
  transfers between devices with their start and end apart: 19, of which 8 were waited for; matrix products, arithmetic and copies ran while one was open for 1% of the time, Pallas kernels for 15%

profile of v1, /device:TPU:14, one launch (start us, length us, event | category | flops | bytes accessed | tf_op | source)
XLA Modules:
  0.0 145.7 jit_solution(8938996163678000746)
XLA Ops:
  0.6 1.3 slice_bitcast_fusion.1
  1.9 2.4 %collective-permute-start = (f32[1024,256]{1,0:T(8,128)S(1)}, f32[1024,256]{1,0:T(8,128)S(1)}, u32[]{:S(2)}, u32[]{:S(2)}) collective-permute-start(f32[1024,256]{1,0:T(8,128)S(1)} %slice_bitcast_fusion.1), channel_id=1, source_target_pairs={{0,1},{1,2},{2,3},{3,0},{4,12},{5,13},{6,14},{7,15},{8,9},{9,10},{... | collective-permute-start | bytes 3145736 | tf_op jit(solution)/shard_map/ppermute | solution.py:201
  4.3 1.3 slice_bitcast_fusion
  5.6 3.5 %collective-permute-start.10 = (f32[1024,256]{1,0:T(8,128)S(1)}, f32[1024,256]{1,0:T(8,128)S(1)}, u32[]{:S(2)}, u32[]{:S(2)}) collective-permute-start(f32[1024,256]{1,0:T(8,128)S(1)} %slice_bitcast_fusion), channel_id=1, source_target_pairs={{0,3},{1,0},{2,1},{3,2},{8,11},{9,8},{10,9},{11,10},{16,19},{17,16... | collective-permute-start | bytes 3145736 | tf_op jit(solution)/shard_map/ppermute | solution.py:201
  9.1 3.6 %collective-permute-start.4 = (f32[1024,256]{1,0:T(8,128)S(1)}, f32[1024,256]{1,0:T(8,128)}, u32[]{:S(2)}, u32[]{:S(2)}) collective-permute-start(f32[1024,256]{1,0:T(8,128)S(1)} %slice_bitcast_fusion), channel_id=1, source_target_pairs={{0,1},{1,2},{2,3},{3,0},{4,12},{5,13},{6,14},{7,15},{8,9},{9,10},{... | collective-permute-start | bytes 3145736 | tf_op jit(solution)/shard_map/ppermute | solution.py:201
  12.7 2.2 %collective-permute-start.8 = (f32[1024,256]{1,0:T(8,128)S(1)}, f32[1024,256]{1,0:T(8,128)S(1)}, u32[]{:S(2)}, u32[]{:S(2)}) collective-permute-start(f32[1024,256]{1,0:T(8,128)S(1)} %slice_bitcast_fusion.1), channel_id=1, source_target_pairs={{0,3},{1,0},{2,1},{3,2},{8,11},{9,8},{10,9},{11,10},{16,19},{17,16... | collective-permute-start | bytes 3145736 | tf_op jit(solution)/shard_map/ppermute | solution.py:201
  14.9 3.7 %collective-permute-done.refs_0_.refs_3_.refs_4_ = f32[1024,256]{1,0:T(8,128)S(1)} collective-permute-done((f32[1024,256]{1,0:T(8,128)S(1)}, f32[1024,256]{1,0:T(8,128)S(1)}, u32[]{:S(2)}, u32[]{:S(2)}) %collective-permute-start) | collective-permute-done | bytes 1048608 | tf_op jit(solution)/shard_map/ppermute | solution.py:201
  18.6 1.0 copy-done
  19.6 3.6 %collective-permute-start.9 = (f32[1024,256]{1,0:T(8,128)S(1)}, f32[1024,256]{1,0:T(8,128)S(1)}, u32[]{:S(2)}, u32[]{:S(2)}) collective-permute-start(f32[1024,256]{1,0:T(8,128)S(1)} %collective-permute-done.refs_0_.refs_3_.refs_4_), channel_id=1, source_target_pairs={{0,1},{1,2},{2,3},{3,0},{8,9},{9,10},{10,11},{11,8},{16,17},{17,18... | collective-permute-start | bytes 3145736 | tf_op jit(solution)/shard_map/ppermute | solution.py:201
  23.2 0.3 collective-permute-done.10.refs_5_
  23.5 2.2 %collective-permute-start.11 = (f32[1024,256]{1,0:T(8,128)S(1)}, f32[1024,256]{1,0:T(8,128)}, u32[]{:S(2)}, u32[]{:S(2)}) collective-permute-start(f32[1024,256]{1,0:T(8,128)S(1)} %collective-permute-done.10.refs_5_), channel_id=1, source_target_pairs={{0,3},{1,0},{2,1},{3,2},{8,11},{9,8},{10,9},{11,10},{16,19},{17,16... | collective-permute-start | bytes 3145736 | tf_op jit(solution)/shard_map/ppermute | solution.py:201
  25.8 4.2 %collective-permute-done.4.refs_4_.refs_7_.refs_0_ = f32[1024,256]{1,0:T(8,128)} collective-permute-done((f32[1024,256]{1,0:T(8,128)S(1)}, f32[1024,256]{1,0:T(8,128)}, u32[]{:S(2)}, u32[]{:S(2)}) %collective-permute-start.4) | collective-permute-done | bytes 1048608 | tf_op jit(solution)/shard_map/ppermute | solution.py:201
  30.0 4.8 %collective-permute-done.8.refs_1_ = f32[1024,256]{1,0:T(8,128)S(1)} collective-permute-done((f32[1024,256]{1,0:T(8,128)S(1)}, f32[1024,256]{1,0:T(8,128)S(1)}, u32[]{:S(2)}, u32[]{:S(2)}) %collective-permute-start.8) | collective-permute-done | bytes 1048608 | tf_op jit(solution)/shard_map/ppermute | solution.py:201
  34.8 6.9 %collective-permute-done.9.refs_2_ = f32[1024,256]{1,0:T(8,128)S(1)} collective-permute-done((f32[1024,256]{1,0:T(8,128)S(1)}, f32[1024,256]{1,0:T(8,128)S(1)}, u32[]{:S(2)}, u32[]{:S(2)}) %collective-permute-start.9) | collective-permute-done | bytes 1048608 | tf_op jit(solution)/shard_map/ppermute | solution.py:201
  41.7 1.0 copy-done.5
  42.7 5.6 %collective-permute-done.11.refs_6_ = f32[1024,256]{1,0:T(8,128)} collective-permute-done((f32[1024,256]{1,0:T(8,128)S(1)}, f32[1024,256]{1,0:T(8,128)}, u32[]{:S(2)}, u32[]{:S(2)}) %collective-permute-start.11) | collective-permute-done | bytes 1048608 | tf_op jit(solution)/shard_map/ppermute | solution.py:201
  48.3 11.8 %shard_map.42.refs_0_.refs_1_.refs_2_.refs_3_.whole = f32[4,1024,256]{2,1,0:T(8,128)} custom-call(f32[2,1024,256]{2,1,0:T(8,128)} %refs_4_.1, f32[1024,256]{1,0:T(8,128)} %copy-done.4, f32[1024,256]{1,0:T(8,128)} %copy-done.5, f32[1024,256]{1,0:T(8,128)} %copy-done, f32[2,1024,256]{2,1,0:T(8,128)} %refs_4_.1, f32[1024,256]{1,0:T(8,128)} %copy-done.3, ...), custom_call_target="tpu_custom_call" | custom-call | flops 6442450944 | bytes 12582912 | tf_op jit(solution)/shard_map/pallas_call | solution.py:52
  60.1 3.3 %collective-permute-start.15 = (f32[4,1024,256]{2,1,0:T(8,128)}, f32[4,1024,256]{2,1,0:T(8,128)}, u32[]{:S(2)}, u32[]{:S(2)}) collective-permute-start(f32[4,1024,256]{2,1,0:T(8,128)} %shard_map.42.refs_0_.refs_1_.refs_2_.refs_3_.whole), channel_id=1, source_target_pairs={{0,4},{1,5},{2,6},{3,7},{8,12},{9,13},{10,14},{11,15},{16,20},{17,... | collective-permute-start | bytes 12582920 | tf_op jit(solution)/shard_map/ppermute | solution.py:201
  63.4 0.7 collective-permute-start.2
  64.1 1.7 %collective-permute-start.5 = (f32[1024,256]{1,0:T(8,128)}, f32[1024,256]{1,0:T(8,128)}, u32[]{:S(2)}, u32[]{:S(2)}) collective-permute-start(f32[1024,256]{1,0:T(8,128)} %collective-permute-done.4.refs_4_.refs_7_.refs_0_), channel_id=1, source_target_pairs={{4,7},{5,4},{6,5},{7,6},{12,15},{13,12},{14,13},{15,14},{20,23},{2... | collective-permute-start | bytes 3145736 | tf_op jit(solution)/shard_map/ppermute | solution.py:201
  65.8 1.6 %collective-permute-start.1 = (f32[1024,256]{1,0:T(8,128)}, f32[1024,256]{1,0:T(8,128)}, u32[]{:S(2)}, u32[]{:S(2)}) collective-permute-start(f32[1024,256]{1,0:T(8,128)} %copy-done), channel_id=1, source_target_pairs={{4,7},{5,4},{6,5},{7,6},{12,15},{13,12},{14,13},{15,14},{20,23},{2... | collective-permute-start | bytes 3145736 | tf_op jit(solution)/shard_map/ppermute | solution.py:201
  67.4 3.3 %collective-permute-start.12 = (f32[4,1024,256]{2,1,0:T(8,128)}, f32[4,1024,256]{2,1,0:T(8,128)}, u32[]{:S(2)}, u32[]{:S(2)}) collective-permute-start(f32[4,1024,256]{2,1,0:T(8,128)} %shard_map.42.refs_0_.refs_1_.refs_2_.refs_3_.whole), channel_id=1, source_target_pairs={{0,12},{1,13},{2,14},{3,15},{8,20},{9,21},{10,22},{11,23},{16,28},... | collective-permute-start | bytes 12582920 | tf_op jit(solution)/shard_map/ppermute | solution.py:201
  70.7 0.0 collective-permute-done.2.refs_3_.refs_7_
  70.7 1.0 copy-done.1
  71.7 1.7 %collective-permute-start.3 = (f32[1024,256]{1,0:T(8,128)S(1)}, f32[1024,256]{1,0:T(8,128)}, u32[]{:S(2)}, u32[]{:S(2)}) collective-permute-start(f32[1024,256]{1,0:T(8,128)S(1)} %collective-permute-done.2.refs_3_.refs_7_), channel_id=1, source_target_pairs={{4,5},{5,6},{6,7},{7,4},{12,13},{13,14},{14,15},{15,12},{20,21},{2... | collective-permute-start | bytes 3145736 | tf_op jit(solution)/shard_map/ppermute | solution.py:201
  73.3 0.0 collective-permute-done.5.refs_5_.refs_1_
  73.3 1.7 %collective-permute-start.7 = (f32[1024,256]{1,0:T(8,128)}, f32[1024,256]{1,0:T(8,128)}, u32[]{:S(2)}, u32[]{:S(2)}) collective-permute-start(f32[1024,256]{1,0:T(8,128)} %collective-permute-done.4.refs_4_.refs_7_.refs_0_), channel_id=1, source_target_pairs={{4,5},{5,6},{6,7},{7,4},{12,13},{13,14},{14,15},{15,12},{20,21},{2... | collective-permute-start | bytes 3145736 | tf_op jit(solution)/shard_map/ppermute | solution.py:201
  75.1 0.0 collective-permute-done.1.refs_1_.refs_5_
  75.1 1.6 %collective-permute-start.6 = (f32[1024,256]{1,0:T(8,128)}, f32[1024,256]{1,0:T(8,128)}, u32[]{:S(2)}, u32[]{:S(2)}) collective-permute-start(f32[1024,256]{1,0:T(8,128)} %collective-permute-done.5.refs_5_.refs_1_), channel_id=1, source_target_pairs={{4,7},{5,4},{6,5},{7,6},{12,15},{13,12},{14,13},{15,14},{20,23},{2... | collective-permute-start | bytes 3145736 | tf_op jit(solution)/shard_map/ppermute | solution.py:201
  76.7 2.7 %shard_map.43 = f32[1024,256]{1,0:T(8,128)} custom-call(f32[1024,256]{1,0:T(8,128)} %copy-done, f32[1024,256]{1,0:T(8,128)} %collective-permute-done.1.refs_1_.refs_5_, f32[1024,256]{1,0:T(8,128)} %collective-permute-done.3.refs_2_.refs_6_, f32[1024,256]{1,0:T(8,128)} %copy-done.1, f32[1024,256]{1,0:T(8,128)} %collective-permute-done.4.refs_4_.refs_7_.refs_0_), custom_call_target="tpu_custom_call" | custom-call | flops 1610612736 | bytes 6291456 | tf_op jit(solution)/shard_map/pallas_call | solution.py:52
  79.4 1.3 collective-permute-start.13
  80.7 0.0 collective-permute-done.7.refs_7_.refs_3_
  80.8 3.4 %shard_map.46 = f32[1024,256]{1,0:T(8,128)} custom-call(f32[1024,256]{1,0:T(8,128)} %collective-permute-done.4.refs_4_.refs_7_.refs_0_, f32[1024,256]{1,0:T(8,128)} %collective-permute-done.5.refs_5_.refs_1_, f32[1024,256]{1,0:T(8,128)} %collective-permute-done.6.refs_6_.refs_2_, f32[1024,256]{1,0:T(8,128)} %collective-permute-done.7.refs_7_.refs_3_, ...), custom_call_target="tpu_custom_call" | custom-call | flops 3221225472 | bytes 10485760 | tf_op jit(solution)/shard_map/pallas_call | solution.py:52
  84.2 1.6 %collective-permute-start.16 = (f32[1024,256]{1,0:T(8,128)}, f32[1024,256]{1,0:T(8,128)}, u32[]{:S(2)}, u32[]{:S(2)}) collective-permute-start(f32[1024,256]{1,0:T(8,128)} %shard_map.46), channel_id=1, source_target_pairs={{12,4},{13,5},{14,6},{15,7},{20,12},{21,13},{22,14},{23,15},{28,20... | collective-permute-start | bytes 3145736 | tf_op jit(solution)/shard_map/ppermute | solution.py:201
  85.8 10.0 %collective-permute-done.13.refs_4_ = f32[1024,256]{1,0:T(8,128)} collective-permute-done((f32[1024,256]{1,0:T(8,128)}, f32[1024,256]{1,0:T(8,128)}, u32[]{:S(2)}, u32[]{:S(2)}) %collective-permute-start.13) | collective-permute-done | bytes 1048608 | tf_op jit(solution)/shard_map/ppermute | solution.py:201
  95.9 4.9 %shard_map.44 = f32[1024,256]{1,0:T(8,128)} custom-call(f32[4,1024,256]{2,1,0:T(8,128)} %shard_map.42.refs_0_.refs_1_.refs_2_.refs_3_.whole, f32[4,1024,256]{2,1,0:T(8,128)} %shard_map.42.refs_0_.refs_1_.refs_2_.refs_3_.whole, f32[4,1024,256]{2,1,0:T(8,128)} %shard_map.42.refs_0_.refs_1_.refs_2_.refs_3_.whole, ...), custom_call_target="tpu_custom_call" | custom-call | flops 1610612736 | bytes 6291456 | tf_op jit(solution)/shard_map/pallas_call | solution.py:52
  100.8 6.8 %collective-permute-start.14 = (f32[1024,256]{1,0:T(8,128)}, f32[1024,256]{1,0:T(8,128)}, u32[]{:S(2)}, u32[]{:S(2)}) collective-permute-start(f32[1024,256]{1,0:T(8,128)} %shard_map.44), channel_id=1, source_target_pairs={{0,4},{1,5},{2,6},{3,7},{8,12},{9,13},{10,14},{11,15},{16,20},{17,... | collective-permute-start | bytes 3145736 | tf_op jit(solution)/shard_map/ppermute | solution.py:201
  107.6 3.5 %shard_map.41.refs_0_.refs_1_.refs_2_.refs_3_.refs_4_.refs_5_.refs_6_.refs_7_ = f32[4,1024,256]{2,1,0:T(8,128)} custom-call(f32[1024,256]{1,0:T(8,128)} %copy-done, f32[1024,256]{1,0:T(8,128)} %collective-permute-done.1.refs_1_.refs_5_, f32[1024,256]{1,0:T(8,128)} %collective-permute-done.3.refs_2_.refs_6_, f32[1024,256]{1,0:T(8,128)} %copy-done.1, ...), custom_call_target="tpu_custom_call" | custom-call | flops 6442450944 | bytes 12582912 | tf_op jit(solution)/shard_map/pallas_call | solution.py:52
  111.1 0.0 collective-permute-done.16.refs_8_
  111.1 3.4 %shard_map.47 = f32[1024,256]{1,0:T(8,128)} custom-call(f32[4,1024,256]{2,1,0:T(8,128)} %collective-permute-done.15.refs_8_.refs_0_.refs_1_.refs_2_.refs_3_, f32[4,1024,256]{2,1,0:T(8,128)} %collective-permute-done.15.refs_8_.refs_0_.refs_1_.refs_2_.refs_3_, f32[4,1024,256]{2,1,0:T(8,128)} %collective-permute-done.15.refs_8_.refs_0_.refs_1_.refs_2_.refs_3_, ...), custom_call_target="tpu_custom_call" | custom-call | flops 3221225472 | bytes 10485760 | tf_op jit(solution)/shard_map/pallas_call | solution.py:52
  114.5 1.3 collective-permute-start.17
  115.8 0.7 slice.13
  116.5 14.9 %collective-permute-start.18 = (f32[8,128]{1,0:T(8,128)S(1)}, f32[8,128]{1,0:T(8,128)S(1)}, u32[]{:S(2)}, u32[]{:S(2)}) collective-permute-start(f32[8,128]{1,0:T(8,128)S(1)} %slice.13), channel_id=1, source_target_pairs={{0,4},{1,5},{2,6},{3,7},{8,12},{9,13},{10,14},{11,15},{16,20},{17,... | collective-permute-start | bytes 12296 | tf_op jit(solution)/shard_map/ppermute | solution.py:201
  131.5 0.0 collective-permute-done.12.refs_4_.refs_5_.refs_6_.refs_7_
  131.5 3.4 %shard_map.45.late = f32[1024,256]{1,0:T(8,128)} custom-call(f32[4,1024,256]{2,1,0:T(8,128)} %shard_map.41.refs_0_.refs_1_.refs_2_.refs_3_.refs_4_.refs_5_.refs_6_.refs_7_, f32[4,1024,256]{2,1,0:T(8,128)} %shard_map.41.refs_0_.refs_1_.refs_2_.refs_3_.refs_4_.refs_5_.refs_6_.refs_7_, ...), custom_call_target="tpu_custom_call" | custom-call | flops 3221225472 | bytes 10485760 | tf_op jit(solution)/shard_map/pallas_call | solution.py:52
  134.9 0.0 collective-permute-done.18.token
  134.9 7.9 %collective-permute-done.17.early = f32[1024,256]{1,0:T(8,128)} collective-permute-done((f32[1024,256]{1,0:T(8,128)}, f32[1024,256]{1,0:T(8,128)}, u32[]{:S(2)}, u32[]{:S(2)}) %collective-permute-start.17) | collective-permute-done | bytes 1048608 | tf_op jit(solution)/shard_map/ppermute | solution.py:201
  142.8 2.9 %shard_map.48 = (f32[1024,256]{1,0:T(8,128)}, f32[1,256]{1,0:T(1,128)}) custom-call(f32[1024,256]{1,0:T(8,128)} %shard_map.45.late, f32[4,1024,256]{2,1,0:T(8,128)} %shard_map.42.refs_0_.refs_1_.refs_2_.refs_3_.whole, f32[1024,256]{1,0:T(8,128)} %collective-permute-done.17.early, f32[1,1024]{1,0:T(1,128)} %bitcast.6, f32[8,128]{1,0:T(8,128)} %copy-done.2), custom_call_target="tpu_custom_call" | custom-call | flops 1048576 | bytes 4194304 | tf_op jit(solution)/shard_map/pallas_call | solution.py:52
  (13 shorter events, 0.0 us)
Async XLA Ops:
  1.9 16.7 %collective-permute-start = (f32[1024,256]{1,0:T(8,128)S(1)}, f32[1024,256]{1,0:T(8,128)S(1)}, u32[]{:S(2)}, u32[]{:S(2)}) collective-permute-start(f32[1024,256]{1,0:T(8,128)S(1)} %slice_bitcast_fusion.1), channel_id=1, source_target_pairs={{0,1},{1,2},{2,3},{3,0},{4,12},{5,13},{6,14},{7,15},{8,9},{9,10},{... | collective-permute-start | bytes 3145736 | tf_op jit(solution)/shard_map/ppermute | solution.py:201
  5.6 17.9 %collective-permute-start.10 = (f32[1024,256]{1,0:T(8,128)S(1)}, f32[1024,256]{1,0:T(8,128)S(1)}, u32[]{:S(2)}, u32[]{:S(2)}) collective-permute-start(f32[1024,256]{1,0:T(8,128)S(1)} %slice_bitcast_fusion), channel_id=1, source_target_pairs={{0,3},{1,0},{2,1},{3,2},{8,11},{9,8},{10,9},{11,10},{16,19},{17,16... | collective-permute-start | bytes 3145736 | tf_op jit(solution)/shard_map/ppermute | solution.py:201
  9.1 20.9 %collective-permute-start.4 = (f32[1024,256]{1,0:T(8,128)S(1)}, f32[1024,256]{1,0:T(8,128)}, u32[]{:S(2)}, u32[]{:S(2)}) collective-permute-start(f32[1024,256]{1,0:T(8,128)S(1)} %slice_bitcast_fusion), channel_id=1, source_target_pairs={{0,1},{1,2},{2,3},{3,0},{4,12},{5,13},{6,14},{7,15},{8,9},{9,10},{... | collective-permute-start | bytes 3145736 | tf_op jit(solution)/shard_map/ppermute | solution.py:201
  12.7 22.1 %collective-permute-start.8 = (f32[1024,256]{1,0:T(8,128)S(1)}, f32[1024,256]{1,0:T(8,128)S(1)}, u32[]{:S(2)}, u32[]{:S(2)}) collective-permute-start(f32[1024,256]{1,0:T(8,128)S(1)} %slice_bitcast_fusion.1), channel_id=1, source_target_pairs={{0,3},{1,0},{2,1},{3,2},{8,11},{9,8},{10,9},{11,10},{16,19},{17,16... | collective-permute-start | bytes 3145736 | tf_op jit(solution)/shard_map/ppermute | solution.py:201
  18.6 1.0 copy-start
  19.6 22.1 %collective-permute-start.9 = (f32[1024,256]{1,0:T(8,128)S(1)}, f32[1024,256]{1,0:T(8,128)S(1)}, u32[]{:S(2)}, u32[]{:S(2)}) collective-permute-start(f32[1024,256]{1,0:T(8,128)S(1)} %collective-permute-done.refs_0_.refs_3_.refs_4_), channel_id=1, source_target_pairs={{0,1},{1,2},{2,3},{3,0},{8,9},{9,10},{10,11},{11,8},{16,17},{17,18... | collective-permute-start | bytes 3145736 | tf_op jit(solution)/shard_map/ppermute | solution.py:201
  23.5 18.2 %copy-start.3 = (f32[1024,256]{1,0:T(8,128)}, f32[1024,256]{1,0:T(8,128)S(1)}, u32[]{:S(2)}) copy-start(f32[1024,256]{1,0:T(8,128)S(1)} %collective-permute-done.10.refs_5_) | copy-start | bytes 3145732
  23.5 24.8 %collective-permute-start.11 = (f32[1024,256]{1,0:T(8,128)S(1)}, f32[1024,256]{1,0:T(8,128)}, u32[]{:S(2)}, u32[]{:S(2)}) collective-permute-start(f32[1024,256]{1,0:T(8,128)S(1)} %collective-permute-done.10.refs_5_), channel_id=1, source_target_pairs={{0,3},{1,0},{2,1},{3,2},{8,11},{9,8},{10,9},{11,10},{16,19},{17,16... | collective-permute-start | bytes 3145736 | tf_op jit(solution)/shard_map/ppermute | solution.py:201
  34.8 7.0 %copy-start.4 = (f32[1024,256]{1,0:T(8,128)}, f32[1024,256]{1,0:T(8,128)S(1)}, u32[]{:S(2)}) copy-start(f32[1024,256]{1,0:T(8,128)S(1)} %collective-permute-done.8.refs_1_) | copy-start | bytes 3145732
  41.7 1.0 copy-start.5
  60.1 20.7 %collective-permute-start.15 = (f32[4,1024,256]{2,1,0:T(8,128)}, f32[4,1024,256]{2,1,0:T(8,128)}, u32[]{:S(2)}, u32[]{:S(2)}) collective-permute-start(f32[4,1024,256]{2,1,0:T(8,128)} %shard_map.42.refs_0_.refs_1_.refs_2_.refs_3_.whole), channel_id=1, source_target_pairs={{0,4},{1,5},{2,6},{3,7},{8,12},{9,13},{10,14},{11,15},{16,20},{17,... | collective-permute-start | bytes 12582920 | tf_op jit(solution)/shard_map/ppermute | solution.py:201
  63.4 7.3 %collective-permute-start.2 = (f32[1024,256]{1,0:T(8,128)}, f32[1024,256]{1,0:T(8,128)S(1)}, u32[]{:S(2)}, u32[]{:S(2)}) collective-permute-start(f32[1024,256]{1,0:T(8,128)} %copy-done), channel_id=1, source_target_pairs={{4,5},{5,6},{6,7},{7,4},{12,13},{13,14},{14,15},{15,12},{20,21},{2... | collective-permute-start | bytes 3145736 | tf_op jit(solution)/shard_map/ppermute | solution.py:201
  64.1 9.2 %collective-permute-start.5 = (f32[1024,256]{1,0:T(8,128)}, f32[1024,256]{1,0:T(8,128)}, u32[]{:S(2)}, u32[]{:S(2)}) collective-permute-start(f32[1024,256]{1,0:T(8,128)} %collective-permute-done.4.refs_4_.refs_7_.refs_0_), channel_id=1, source_target_pairs={{4,7},{5,4},{6,5},{7,6},{12,15},{13,12},{14,13},{15,14},{20,23},{2... | collective-permute-start | bytes 3145736 | tf_op jit(solution)/shard_map/ppermute | solution.py:201
  65.8 9.3 %collective-permute-start.1 = (f32[1024,256]{1,0:T(8,128)}, f32[1024,256]{1,0:T(8,128)}, u32[]{:S(2)}, u32[]{:S(2)}) collective-permute-start(f32[1024,256]{1,0:T(8,128)} %copy-done), channel_id=1, source_target_pairs={{4,7},{5,4},{6,5},{7,6},{12,15},{13,12},{14,13},{15,14},{20,23},{2... | collective-permute-start | bytes 3145736 | tf_op jit(solution)/shard_map/ppermute | solution.py:201
  67.4 64.1 %collective-permute-start.12 = (f32[4,1024,256]{2,1,0:T(8,128)}, f32[4,1024,256]{2,1,0:T(8,128)}, u32[]{:S(2)}, u32[]{:S(2)}) collective-permute-start(f32[4,1024,256]{2,1,0:T(8,128)} %shard_map.42.refs_0_.refs_1_.refs_2_.refs_3_.whole), channel_id=1, source_target_pairs={{0,12},{1,13},{2,14},{3,15},{8,20},{9,21},{10,22},{11,23},{16,28},... | collective-permute-start | bytes 12582920 | tf_op jit(solution)/shard_map/ppermute | solution.py:201
  70.7 1.0 copy-start.1
  71.7 5.0 %collective-permute-start.3 = (f32[1024,256]{1,0:T(8,128)S(1)}, f32[1024,256]{1,0:T(8,128)}, u32[]{:S(2)}, u32[]{:S(2)}) collective-permute-start(f32[1024,256]{1,0:T(8,128)S(1)} %collective-permute-done.2.refs_3_.refs_7_), channel_id=1, source_target_pairs={{4,5},{5,6},{6,7},{7,4},{12,13},{13,14},{14,15},{15,12},{20,21},{2... | collective-permute-start | bytes 3145736 | tf_op jit(solution)/shard_map/ppermute | solution.py:201
  73.3 7.4 %collective-permute-start.7 = (f32[1024,256]{1,0:T(8,128)}, f32[1024,256]{1,0:T(8,128)}, u32[]{:S(2)}, u32[]{:S(2)}) collective-permute-start(f32[1024,256]{1,0:T(8,128)} %collective-permute-done.4.refs_4_.refs_7_.refs_0_), channel_id=1, source_target_pairs={{4,5},{5,6},{6,7},{7,4},{12,13},{13,14},{14,15},{15,12},{20,21},{2... | collective-permute-start | bytes 3145736 | tf_op jit(solution)/shard_map/ppermute | solution.py:201
  75.1 5.7 %collective-permute-start.6 = (f32[1024,256]{1,0:T(8,128)}, f32[1024,256]{1,0:T(8,128)}, u32[]{:S(2)}, u32[]{:S(2)}) collective-permute-start(f32[1024,256]{1,0:T(8,128)} %collective-permute-done.5.refs_5_.refs_1_), channel_id=1, source_target_pairs={{4,7},{5,4},{6,5},{7,6},{12,15},{13,12},{14,13},{15,14},{20,23},{2... | collective-permute-start | bytes 3145736 | tf_op jit(solution)/shard_map/ppermute | solution.py:201
  79.4 16.4 %collective-permute-start.13 = (f32[1024,256]{1,0:T(8,128)}, f32[1024,256]{1,0:T(8,128)}, u32[]{:S(2)}, u32[]{:S(2)}) collective-permute-start(f32[1024,256]{1,0:T(8,128)} %shard_map.43), channel_id=1, source_target_pairs={{4,504},{5,505},{6,506},{7,507},{12,0},{13,1},{14,2},{15,3},{20,8}... | collective-permute-start | bytes 3145736 | tf_op jit(solution)/shard_map/ppermute | solution.py:201
  84.2 26.9 %collective-permute-start.16 = (f32[1024,256]{1,0:T(8,128)}, f32[1024,256]{1,0:T(8,128)}, u32[]{:S(2)}, u32[]{:S(2)}) collective-permute-start(f32[1024,256]{1,0:T(8,128)} %shard_map.46), channel_id=1, source_target_pairs={{12,4},{13,5},{14,6},{15,7},{20,12},{21,13},{22,14},{23,15},{28,20... | collective-permute-start | bytes 3145736 | tf_op jit(solution)/shard_map/ppermute | solution.py:201
  100.8 30.7 %collective-permute-start.14 = (f32[1024,256]{1,0:T(8,128)}, f32[1024,256]{1,0:T(8,128)}, u32[]{:S(2)}, u32[]{:S(2)}) collective-permute-start(f32[1024,256]{1,0:T(8,128)} %shard_map.44), channel_id=1, source_target_pairs={{0,4},{1,5},{2,6},{3,7},{8,12},{9,13},{10,14},{11,15},{16,20},{17,... | collective-permute-start | bytes 3145736 | tf_op jit(solution)/shard_map/ppermute | solution.py:201
  114.5 28.2 %collective-permute-start.17 = (f32[1024,256]{1,0:T(8,128)}, f32[1024,256]{1,0:T(8,128)}, u32[]{:S(2)}, u32[]{:S(2)}) collective-permute-start(f32[1024,256]{1,0:T(8,128)} %shard_map.47), channel_id=1, source_target_pairs={{4,8},{5,9},{6,10},{7,11},{12,16},{13,17},{14,18},{15,19},{20,24},... | collective-permute-start | bytes 3145736 | tf_op jit(solution)/shard_map/ppermute | solution.py:201
  116.5 18.4 %collective-permute-start.18 = (f32[8,128]{1,0:T(8,128)S(1)}, f32[8,128]{1,0:T(8,128)S(1)}, u32[]{:S(2)}, u32[]{:S(2)}) collective-permute-start(f32[8,128]{1,0:T(8,128)S(1)} %slice.13), channel_id=1, source_target_pairs={{0,4},{1,5},{2,6},{3,7},{8,12},{9,13},{10,14},{11,15},{16,20},{17,... | collective-permute-start | bytes 12296 | tf_op jit(solution)/shard_map/ppermute | solution.py:201
  134.9 7.9 %copy-start.2 = (f32[8,128]{1,0:T(8,128)}, f32[8,128]{1,0:T(8,128)S(1)}, u32[]{:S(2)}) copy-start(f32[8,128]{1,0:T(8,128)S(1)} %collective-permute-done.18.token) | copy-start | bytes 12292

commit v2 on v1

--- a/solution.py
+++ b/solution.py
@@ -34,18 +34,23 @@
     return dot(high, v_high) + (dot(high, v_low) + dot(low, v_high))
 
 
-def tile_product(x, left_refs, v_high, v_low):
-    total = None
-    for r, ref in enumerate(left_refs):
-        depth = ref.shape[1]
-        rows = pl.ds(pl.multiple_of(lax.rem(x + r, len(left_refs)) * depth, depth), depth)
-        part = dot3(*high_low(ref[...]), v_high[rows, :], v_low[rows, :])
-        total = part if total is None else total + part
-    return total
-
-
-def put(v_high, v_low, where, value):
-    v_high[where], v_low[where] = high_low(value)
+def put(v, x, block, columns, value):
+    depth = value.shape[0]
+    n = v.shape[0] // (3 * depth)
+    at = lax.rem(block - x + n, n) * depth
+    high, low = high_low(value)
+    for part, a in enumerate((high, low, high)):
+        v[pl.ds(pl.multiple_of(at + part * n * depth, depth), depth), columns] = a
+
+
+def put_all(v, x, columns, ref, depth):
+    for block in range(ref.shape[0] // depth):
+        put(v, x, block, columns, ref[block * depth : (block + 1) * depth, :])
+
+
+def tile_product(left_refs, v):
+    high, low = high_low(jnp.concatenate([ref[...] for ref in left_refs], axis=1))
+    return jnp.dot(jnp.concatenate([high, high, low], axis=1), v[...], preferred_element_type=jnp.float32)
 
 
 def call_kernel(kernel, out_shape, grid, specs, out_specs, scratch, args, flops, traffic):
@@ -58,15 +63,16 @@
         scratch_shapes=scratch,
         compiler_params=pltpu.CompilerParams(vmem_limit_bytes=67_000_000),
         cost_estimate=pl.CostEstimate(flops=flops, bytes_accessed=traffic, transcendentals=0),
-    )(*args)
+    )(*[pltpu.with_memory_space_constraint(a, pltpu.HBM) for a in args])
 
 
 def only(on, index):
     return lambda i: jnp.where(place()[1] == on, index(i), 0)
 
 
-def product_kernel(n_left, n_right, width, on, *refs):
-    lefts, rights, (out, v_high, v_low) = refs[:n_left], refs[n_left : n_left + n_right], refs[n_left + n_right :]
+def product_kernel(n_left, picks, width, on, *refs):
+    n_right = len(picks)
+    lefts, rights, (out, held, v, sems) = refs[:n_left], refs[n_left : n_left + n_right], refs[n_left + n_right :]
     i = pl.program_id(0)
     _, core, x = place()
 
@@ -74,10 +80,16 @@
     def _():
         @pl.when(i == 0)
         def _():
+            copies = []
             for j, ref in enumerate(rights):
-                put(v_high, v_low, (slice(None), slice(j * width, (j + 1) * width)), ref[...])
-
-        total = tile_product(x, lefts, v_high, v_low)
+                source = ref if picks[j] is None else ref.at[picks[j]]
+                copies.append(pltpu.make_async_copy(source, held.at[j], sems.at[j]))
+                copies[j].start()
+            for j, copy in enumerate(copies):
+                copy.wait()
+                put_all(v, x, slice(j * width, (j + 1) * width), held.at[j], lefts[0].shape[1])
+
+        total = tile_product(lefts, v)
         for j in range(n_right):
             out[j] = total[:, j * width : (j + 1) * width]
 
@@ -86,13 +98,18 @@
     rows, depth = left[0][0].shape[-2:]
     width = right[0][0].shape[-1]
     n, full = len(right), len(left) * depth
+    step = only(on, lambda i: i)
     return call_kernel(
-        functools.partial(product_kernel, len(left), n, width, on),
+        functools.partial(product_kernel, len(left), [p[1] for p in right], width, on),
         jax.ShapeDtypeStruct((n, rows, width), jnp.float32),
         rows // TILE,
-        [spec(p, TILE, only(on, lambda i: i)) for p in left] + [spec(p, rows, lambda i: 0) for p in right],
-        pl.BlockSpec((n, TILE, width), lambda i: (0, only(on, lambda i: i)(i), 0)),
-        [pltpu.VMEM((full, n * width), jnp.bfloat16)] * 2,
+        [spec(p, TILE, step) for p in left] + [pl.BlockSpec(memory_space=pl.ANY)] * n,
+        pl.BlockSpec((n, TILE, width), lambda i: (0, step(i), 0)),
+        [
+            pltpu.VMEM((n, rows, width), jnp.float32),
+            pltpu.VMEM((3 * full, n * width), jnp.bfloat16),
+            pltpu.SemaphoreType.DMA((n,)),
+        ],
         [p[0] for p in left + right],
         6 * rows * full * n * width,
         4 * (rows * full + 2 * n * rows * width),
@@ -101,38 +118,45 @@
 
 def chain_kernel(counts, tiles, on, passes, *refs):
     n_left = sum(counts)
-    lefts, (right, out, v_high, v_low) = refs[:n_left], refs[n_left:]
+    lefts, (right, out, v) = refs[:n_left], refs[n_left:]
     i = pl.program_id(0)
     k, core, x = place()
-    own = pl.ds(pl.multiple_of(lax.rem(i, tiles) * CHAIN_TILE, CHAIN_TILE), CHAIN_TILE)
+    depth = lefts[0].shape[1]
+    blocks = CHAIN_TILE // depth
+    tile = lax.rem(i, tiles)
     active = core == on
 
     @pl.when(active & (i == 0))
     def _():
-        put(v_high, v_low, 0, right[...])
+        put_all(v.at[0], x, slice(None), right, depth)
 
     at = 0
     for n, count in enumerate(counts):
         here = lefts[at : at + count]
         at += count
         now, later, last = n % 2, (n + 1) % 2, n + 1 == len(counts)
-
-        def keep(total, later=later, last=last):
+        mine = active & (i >= n * tiles) & (i < (n + 1) * tiles)
+        skipped = passes[n] & (k == 0)
+
+        @pl.when(mine & jnp.logical_not(skipped))
+        def _(here=here, now=now, later=later, last=last):
+            total = tile_product(here, v.at[now])
             if last:
                 out[...] = total
             else:
-                put(v_high, v_low, (later, own), total)
-
-        mine = active & (i >= n * tiles) & (i < (n + 1) * tiles)
-        skipped = passes[n] & (k == 0)
-
-        @pl.when(mine & jnp.logical_not(skipped))
-        def _(here=here, now=now, keep=keep):
-            keep(tile_product(x, here, v_high.at[now], v_low.at[now]))
+                for h in range(blocks):
+                    put(v.at[later], x, tile * blocks + h, slice(None), total[h * depth : (h + 1) * depth])
 
         @pl.when(mine & skipped)
-        def _(now=now, keep=keep):
-            keep(v_high[now, own, :].astype(jnp.float32) + v_low[now, own, :].astype(jnp.float32))
+        def _(now=now, later=later, last=last):
+            for h in range(blocks):
+                block = lax.rem(tile * blocks + h - x + count, count) * depth
+                high = v[now, pl.ds(pl.multiple_of(block, depth), depth), :].astype(jnp.float32)
+                low = v[now, pl.ds(pl.multiple_of(block + count * depth, depth), depth), :].astype(jnp.float32)
+                if last:
+                    out[h * depth : (h + 1) * depth, :] = high + low
+                else:
+                    put(v.at[later], x, tile * blocks + h, slice(None), high + low)
 
 
 def chain(lefts, right, on, passes):
@@ -148,10 +172,68 @@
         n * tiles,
         specs + [spec(right, rows, lambda i: 0)],
         pl.BlockSpec((CHAIN_TILE, width), lambda i: (only(on, lambda i: jnp.maximum(i - (n - 1) * tiles, 0))(i), 0)),
-        [pltpu.VMEM((2, rows, width), jnp.bfloat16)] * 2,
+        [pltpu.VMEM((2, 3 * rows, width), jnp.bfloat16)],
         [p[0] for left in lefts for p in left] + [right[0]],
         6 * n * rows * rows * width,
         4 * (n * rows * rows + 2 * rows * width),
+    )
+
+
+def pair_kernel(places, n_x, done, *refs):
+    lefts, rights, refs = refs[: len(places)], refs[len(places) : len(places) + 2], refs[len(places) + 2 :]
+    i = pl.program_id(0)
+    k, core, x = place()
+    depth, width, n = lefts[0].shape[1], rights[0].shape[1], len(places)
+    v = refs[-1]
+
+    @pl.when(core == 1)
+    def _():
+        @pl.when(i == 0)
+        def _():
+            for j, ref in enumerate(rights):
+                for at, r in enumerate(places):
+                    block = lax.rem(x + r, n_x) * depth
+                    high, low = high_low(ref[pl.ds(pl.multiple_of(block, depth), depth), :])
+                    for part, a in enumerate((high, low, high)):
+                        row = (part * n + at) * depth
+                        v[row : row + depth, j * width : (j + 1) * width] = a
+
+        total = tile_product(lefts, v)
+        if done:
+            begun, passed, step, ahead = refs[:4]
+            step[...] = jnp.where(k == 0, passed[...], total[:, :width] + begun[0])
+            ahead[...] = total[:, width:] + begun[1]
+        else:
+            refs[0][0] = total[:, :width]
+            refs[0][1] = total[:, width:]
+
+
+def pair(left, right, begun=None, passed=None):
+    first = next(iter(left.values()))
+    rows, depth = first[0].shape[-2:]
+    width = right[0][0].shape[-1]
+    n = len(left)
+    both = pl.BlockSpec((2, CHAIN_TILE, width), lambda i: (0, i, 0))
+    one = pl.BlockSpec((CHAIN_TILE, width), lambda i: (i, 0))
+    f32 = jnp.float32
+    specs = [spec(p, CHAIN_TILE, lambda i: i) for p in left.values()] + [spec(p, rows, lambda i: 0) for p in right]
+    args = [p[0] for p in [*left.values(), *right]]
+    if begun is None:
+        out, out_specs = jax.ShapeDtypeStruct((2, rows, width), f32), both
+    else:
+        out, out_specs = [jax.ShapeDtypeStruct((rows, width), f32)] * 2, [one, one]
+        specs += [both, spec(passed, CHAIN_TILE, lambda i: i)]
+        args += [begun, passed[0]]
+    return call_kernel(
+        functools.partial(pair_kernel, tuple(left), rows // depth, begun is not None),
+        out,
+        rows // CHAIN_TILE,
+        specs,
+        out_specs,
+        [pltpu.VMEM((3 * n * depth, 2 * width), jnp.bfloat16)],
+        args,
+        12 * rows * n * depth * width,
+        4 * (rows * n * depth + 6 * rows * width),
     )
 
 
@@ -172,7 +254,15 @@
 
 def finish(late, whole, early, start, token):
     rows, width = late.shape
-    tiles = [spec(p, CHAIN_TILE, lambda i: i) for p in ((late, None), whole, (early, None))]
+
+    def used(role):
+        def index(i):
+            k, core, _ = place()
+            return jnp.where(jnp.where(core == 1, 0, jnp.where(k == 0, 1, 2)) == role, i, 0)
+
+        return index
+
+    tiles = [spec(p, CHAIN_TILE, used(n)) for n, p in enumerate(((late, None), whole, (early, None)))]
     return call_kernel(
         functools.partial(finish_kernel, float(rows)),
         [jax.ShapeDtypeStruct((rows, width), jnp.float32), jax.ShapeDtypeStruct((1, width), jnp.float32)],
@@ -190,9 +280,9 @@
     n_tm, n_x = lax.axis_size("tm"), lax.axis_size("panel")
     n_chips = n_tm // 2
 
-    def send(a, even=None, odd=None, wrap=False):
+    def send(a, even=None, odd=None, wrap=False, since=0):
         pairs = []
-        for kk in range(n_chips):
+        for kk in range(since, n_chips):
             for cc, to in enumerate((even, odd)):
                 for xx in range(n_x):
                     if to is not None and (wrap or 0 <= kk + to[0] < n_chips):
@@ -207,14 +297,15 @@
     a_right = send(a, (0, 0, -1))
     a_far = send(a_left, (0, 0, 1))
     c_far = send(c_right, (0, 0, -1))
-    token = send(c_left[:8, :128], (0, 1, 0))
+    token = c_left[:8, :128]
+    token = send(token, (0, 1, 0))
     a_odd, c_odd = a_left, c_left
+    c_odd_left = send(c_odd, None, (0, 1, 1), since=1)
+    a_odd_right = send(a_odd, None, (0, 1, -1))
+    c_odd_right = send(c_odd, None, (0, 1, -1), since=1)
+    c_odd_far = send(c_odd_left, None, (0, 1, 1), since=1)
+    a_odd_far = send(a_odd_right, None, (0, 1, -1))
     a_odd_left = send(a_odd, None, (0, 1, 1))
-    a_odd_right = send(a_odd, None, (0, 1, -1))
-    c_odd_right = send(c_odd, None, (0, 1, -1))
-    a_odd_far = send(a_odd_left, None, (0, 1, 1))
-    c_odd_left = send(c_odd, None, (0, 1, 1))
-    c_odd_far = send(c_odd_right, None, (0, 1, -1))
 
     def panels(own, right, far, left):
         return [own, (right, None), (far, None), (left, None)]
@@ -229,16 +320,19 @@
     even_before = stacked(send(even, (1, 1, 0)))
     left = panels((a_odd, None), a_odd_right, a_odd_far, a_odd_left)
     right = panels((c_odd, None), c_odd_right, c_odd_far, c_odd_left)
-    step = chain([right, left], even_here[0], 1, (True, True))
+    here = even_here[0]
+    inner = chain([right], here, 1, (False,))
+    pairs = [(inner, None), right[0]]
+    begun = pair({0: left[0], 1: left[1]}, pairs)
+    step, ahead = pair({2: left[2], 3: left[3]}, pairs, begun, here)
     there = send(step, None, (-1, 1, 0))
-    ahead = chain([left], right[0], 1, (False,))
-    ahead = send(ahead, None, (-1, 0, 0), wrap=True)
-    odd = stacked(product(left, right, 1))
-    cross = chain([stacked(even)], (ahead, None), 0, (False,))
-    cross = send(cross, (0, 1, 0))
+    own = ahead
+    ahead = send(ahead, None, (-1, 1, 0), wrap=True)
+    rest = product(left, right[1:], 1)
+    odd = [(own, None)] + [(rest, j) for j in range(n_x - 1)]
     step = chain([even_here, odd], (there, None), 1, (False, True))
     early = send(step, None, (1, 0, 0))
-    late = chain([odd, even_before], (cross, None), 1, (True, True))
+    late = chain([even_here, odd, even_before], (ahead, None), 1, (False, True, True))
     window, occupancy = finish(late, (even, 0), early, start_weights[None, :], token)
     return window[None], occupancy
 

time: 146 us -> 146 us (level)
  the two profiles are of different devices: /device:TPU:14 before, /device:TPU:1 now
where the time goes in v2:
time: 146 us; the launch traced here: 145 us
  starting transfers between devices  53.1 us (36%)
  Pallas kernels  49.2 us (34%)
  waiting for transfers between devices  34.4 us (24%)
  local copies, waits for them, and re-layouts  7.84 us (5%)
    ppermute x18, starting transfers between devices, send(): return lax.ppermute(a, ('tm', 'panel'), pairs)  53.1 us
    pallas_call x8, Pallas kernels, call_kernel(): pl.pallas_call(kernel, out_shape=out_shape, grid=(grid,), in_specs=specs,...  49.2 us
    ppermute x18, waiting for transfers between devices, send(): return lax.ppermute(a, ('tm', 'panel'), pairs)  34.4 us
    unnamed x16, local copies, waits for them, and re-layouts  4.57 us
  transfers between devices with their start and end apart: 18, of which 4 were waited for; matrix products, arithmetic and copies ran while one was open for 1% of the time, Pallas kernels for 30%

profile of v2, /device:TPU:1, one launch (start us, length us, event | category | flops | bytes accessed | tf_op | source)
XLA Modules:
  0.0 145.3 jit_solution(16402747112632188514)
XLA Ops:
  0.6 1.3 slice_bitcast_fusion.1
  1.9 4.0 %collective-permute-start.1 = (f32[1024,256]{1,0:T(8,128)S(1)}, f32[1024,256]{1,0:T(8,128)S(1)}, u32[]{:S(2)}, u32[]{:S(2)}) collective-permute-start(f32[1024,256]{1,0:T(8,128)S(1)} %slice_bitcast_fusion.1), channel_id=1, source_target_pairs={{0,1},{1,2},{2,3},{3,0},{4,12},{5,13},{6,14},{7,15},{8,9},{9,10},{... | collective-permute-start | bytes 3145736 | tf_op jit(solution)/shard_map/ppermute | solution.py:291
  6.0 1.3 slice_bitcast_fusion
  7.3 0.7 collective-permute-start.3
  8.0 3.2 %collective-permute-start.5 = (f32[1024,256]{1,0:T(8,128)S(1)}, f32[1024,256]{1,0:T(8,128)}, u32[]{:S(2)}, u32[]{:S(2)}) collective-permute-start(f32[1024,256]{1,0:T(8,128)S(1)} %slice_bitcast_fusion), channel_id=1, source_target_pairs={{0,1},{1,2},{2,3},{3,0},{4,12},{5,13},{6,14},{7,15},{8,9},{9,10},{... | collective-permute-start | bytes 3145736 | tf_op jit(solution)/shard_map/ppermute | solution.py:291
  11.2 0.7 collective-permute-start
  11.9 16.6 %collective-permute-done.1.refs_3_.refs_0_ = f32[1024,256]{1,0:T(8,128)S(1)} collective-permute-done((f32[1024,256]{1,0:T(8,128)S(1)}, f32[1024,256]{1,0:T(8,128)S(1)}, u32[]{:S(2)}, u32[]{:S(2)}) %collective-permute-start.1) | collective-permute-done | bytes 1048608 | tf_op jit(solution)/shard_map/ppermute | solution.py:291
  28.5 0.7 collective-permute-start.2
  29.2 1.6 %collective-permute-start.4 = (f32[1024,256]{1,0:T(8,128)S(1)}, f32[1024,256]{1,0:T(8,128)}, u32[]{:S(2)}, u32[]{:S(2)}) collective-permute-start(f32[1024,256]{1,0:T(8,128)S(1)} %collective-permute-done.3.refs_5_), channel_id=1, source_target_pairs={{0,3},{1,0},{2,1},{3,2},{8,11},{9,8},{10,9},{11,10},{16,19},{17,16... | collective-permute-start | bytes 3145736 | tf_op jit(solution)/shard_map/ppermute | solution.py:291
  30.9 9.0 %collective-permute-done.5.refs_7_.refs_0_.refs_3_ = f32[1024,256]{1,0:T(8,128)} collective-permute-done((f32[1024,256]{1,0:T(8,128)S(1)}, f32[1024,256]{1,0:T(8,128)}, u32[]{:S(2)}, u32[]{:S(2)}) %collective-permute-start.5) | collective-permute-done | bytes 1048608 | tf_op jit(solution)/shard_map/ppermute | solution.py:291
  39.8 0.0 collective-permute-done.refs_1_
  39.9 0.0 collective-permute-done.2.refs_2_
  39.9 0.9 copy-done.6
  40.8 1.0 copy-done.7
  41.8 0.0 collective-permute-done.4.refs_6_
  41.8 2.2 %shard_map.41.whole = f32[4,1024,256]{2,1,0:T(8,128)} custom-call(f32[2,1024,256]{2,1,0:T(8,128)} %refs_4_.1, f32[1024,256]{1,0:T(8,128)} %copy-done.6, f32[1024,256]{1,0:T(8,128)} %copy-done.7, f32[1024,256]{1,0:T(8,128)} %copy-done.3, f32[2,1024,256]{2,1,0:T(8,128)} %refs_4_.1, f32[1024,256]{1,0:T(8,128)} %copy-done.5, ...), custom_call_target="tpu_custom_call" | custom-call | flops 6442450944 | bytes 12582912 | tf_op jit(solution)/shard_map/pallas_call | solution.py:57
  44.1 1.3 collective-permute-start.6
  45.4 0.7 collective-permute-start.11
  46.1 0.7 collective-permute-start.10
  46.8 4.4 %collective-permute-start.7 = (f32[1024,256]{1,0:T(8,128)}, f32[1024,256]{1,0:T(8,128)}, u32[]{:S(2)}, u32[]{:S(2)}) collective-permute-start(f32[1024,256]{1,0:T(8,128)} %copy-done.3), channel_id=1, source_target_pairs={{4,7},{5,4},{6,5},{7,6},{12,15},{13,12},{14,13},{15,14},{20,23},{2... | collective-permute-start | bytes 3145736 | tf_op jit(solution)/shard_map/ppermute | solution.py:291
  51.2 2.6 %collective-permute-start.13 = (f32[4,1024,256]{2,1,0:T(8,128)}, f32[4,1024,256]{2,1,0:T(8,128)}, u32[]{:S(2)}, u32[]{:S(2)}) collective-permute-start(f32[4,1024,256]{2,1,0:T(8,128)} %shard_map.41.whole), channel_id=1, source_target_pairs={{0,12},{1,13},{2,14},{3,15},{8,20},{9,21},{10,22},{11,23},{16,28},... | collective-permute-start | bytes 12582920 | tf_op jit(solution)/shard_map/ppermute | solution.py:291
  53.9 0.0 collective-permute-done.11.refs_3_.refs_6_
  53.9 1.1 copy-done
  54.9 0.7 collective-permute-start.12
  55.7 0.0 copy-start.1
  55.7 1.9 %collective-permute-start.9 = (f32[1024,256]{1,0:T(8,128)}, f32[1024,256]{1,0:T(8,128)}, u32[]{:S(2)}, u32[]{:S(2)}) collective-permute-start(f32[1024,256]{1,0:T(8,128)} %copy-done.3), channel_id=1, source_target_pairs={{4,5},{5,6},{6,7},{7,4},{12,13},{13,14},{14,15},{15,12},{20,21},{2... | collective-permute-start | bytes 3145736 | tf_op jit(solution)/shard_map/ppermute | solution.py:291
  57.6 5.6 %collective-permute-done.7.refs_1_ = f32[1024,256]{1,0:T(8,128)} collective-permute-done((f32[1024,256]{1,0:T(8,128)}, f32[1024,256]{1,0:T(8,128)}, u32[]{:S(2)}, u32[]{:S(2)}) %collective-permute-start.7) | collective-permute-done | bytes 1048608 | tf_op jit(solution)/shard_map/ppermute | solution.py:291
  63.3 5.0 %collective-permute-start.8 = (f32[1024,256]{1,0:T(8,128)}, f32[1024,256]{1,0:T(8,128)}, u32[]{:S(2)}, u32[]{:S(2)}) collective-permute-start(f32[1024,256]{1,0:T(8,128)} %collective-permute-done.7.refs_1_), channel_id=1, source_target_pairs={{4,7},{5,4},{6,5},{7,6},{12,15},{13,12},{14,13},{15,14},{20,23},{2... | collective-permute-start | bytes 3145736 | tf_op jit(solution)/shard_map/ppermute | solution.py:291
  68.3 0.0 collective-permute-done.12.refs_2_.refs_5_
  68.3 1.0 copy-done.2
  69.3 3.2 %collective-permute-done.6.refs_4_.refs_5_.refs_0_.refs_1_.refs_2_.refs_3_ = f32[4,1024,256]{2,1,0:T(8,128)} collective-permute-done((f32[4,1024,256]{2,1,0:T(8,128)}, f32[4,1024,256]{2,1,0:T(8,128)}, u32[]{:S(2)}, u32[]{:S(2)}) %collective-permute-start.6) | collective-permute-done | bytes 4194336 | tf_op jit(solution)/shard_map/ppermute | solution.py:291
  72.5 5.0 %shard_map.42.refs_2_ = f32[1024,256]{1,0:T(8,128)} custom-call(f32[1024,256]{1,0:T(8,128)} %collective-permute-done.5.refs_7_.refs_0_.refs_3_, f32[1024,256]{1,0:T(8,128)} %copy-done.1, f32[1024,256]{1,0:T(8,128)} %copy-done.2, f32[1024,256]{1,0:T(8,128)} %copy-done, f32[4,1024,256]{2,1,0:T(8,128)} %collective-permute-done.6.refs_4_.refs_5_.refs_0_.refs_1_.refs_2_.refs_3_), custom_call_target="tpu_custom_call" | custom-call | flops 1610612736 | bytes 6291456 | tf_op jit(solution)/shard_map/pallas_call | solution.py:57
  77.4 5.0 %shard_map.43.refs_4_ = f32[2,1024,256]{2,1,0:T(8,128)} custom-call(f32[1024,256]{1,0:T(8,128)} %copy-done.3, f32[1024,256]{1,0:T(8,128)} %collective-permute-done.7.refs_1_, f32[1024,256]{1,0:T(8,128)} %shard_map.42.refs_2_, f32[1024,256]{1,0:T(8,128)} %collective-permute-done.5.refs_7_.refs_0_.refs_3_), custom_call_target="tpu_custom_call" | custom-call | flops 1610612736 | bytes 8388608 | tf_op jit(solution)/shard_map/pallas_call | solution.py:57
  82.4 0.0 collective-permute-done.9.refs_1_.refs_3_
  82.4 0.0 collective-permute-done.8.refs_0_.refs_2_
  82.4 5.5 %shard_map.44 = (f32[1024,256]{1,0:T(8,128)}, f32[1024,256]{1,0:T(8,128)}) custom-call(f32[1024,256]{1,0:T(8,128)} %collective-permute-done.8.refs_0_.refs_2_, f32[1024,256]{1,0:T(8,128)} %collective-permute-done.9.refs_1_.refs_3_, f32[1024,256]{1,0:T(8,128)} %shard_map.42.refs_2_, f32[1024,256]{1,0:T(8,128)} %collective-permute-done.5.refs_7_.refs_0_.refs_3_, ...), custom_call_target="tpu_custom_call" | custom-call | flops 1610612736 | bytes 8388608 | tf_op jit(solution)/shard_map/pallas_call | solution.py:57
  88.0 1.3 collective-permute-start.15
  89.3 19.6 %collective-permute-start.14 = (f32[1024,256]{1,0:T(8,128)}, f32[1024,256]{1,0:T(8,128)}, u32[]{:S(2)}, u32[]{:S(2)}) collective-permute-start(f32[1024,256]{1,0:T(8,128)} %get-tuple-element.6.refs_4_), channel_id=1, source_target_pairs={{4,508},{5,509},{6,510},{7,511},{12,4},{13,5},{14,6},{15,7},{20,12... | collective-permute-start | bytes 3145736 | tf_op jit(solution)/shard_map/ppermute | solution.py:291
  108.8 10.3 %shard_map.45.refs_5_.refs_6_.refs_7_ = f32[3,1024,256]{2,1,0:T(8,128)} custom-call(f32[1024,256]{1,0:T(8,128)} %copy-done.3, f32[1024,256]{1,0:T(8,128)} %collective-permute-done.7.refs_1_, f32[1024,256]{1,0:T(8,128)} %collective-permute-done.8.refs_0_.refs_2_, f32[1024,256]{1,0:T(8,128)} %collective-permute-done.9.refs_1_.refs_3_, f32[1024,256]{1,0:T(8,128)} %copy-done.1, ...), custom_call_target="tpu_custom_call" | custom-call | flops 4831838208 | bytes 10485760 | tf_op jit(solution)/shard_map/pallas_call | solution.py:57
  119.1 7.8 %shard_map.47 = f32[1024,256]{1,0:T(8,128)} custom-call(f32[4,1024,256]{2,1,0:T(8,128)} %collective-permute-done.6.refs_4_.refs_5_.refs_0_.refs_1_.refs_2_.refs_3_, f32[4,1024,256]{2,1,0:T(8,128)} %collective-permute-done.6.refs_4_.refs_5_.refs_0_.refs_1_.refs_2_.refs_3_, ...), custom_call_target="tpu_custom_call" | custom-call | flops 3221225472 | bytes 10485760 | tf_op jit(solution)/shard_map/pallas_call | solution.py:57
  126.9 2.3 %collective-permute-start.16 = (f32[1024,256]{1,0:T(8,128)}, f32[1024,256]{1,0:T(8,128)}, u32[]{:S(2)}, u32[]{:S(2)}) collective-permute-start(f32[1024,256]{1,0:T(8,128)} %shard_map.47), channel_id=1, source_target_pairs={{4,8},{5,9},{6,10},{7,11},{12,16},{13,17},{14,18},{15,19},{20,24},... | collective-permute-start | bytes 3145736 | tf_op jit(solution)/shard_map/ppermute | solution.py:291
  129.2 0.7 slice.13
  129.9 1.5 %collective-permute-start.17 = (f32[8,128]{1,0:T(8,128)S(1)}, f32[8,128]{1,0:T(8,128)S(1)}, u32[]{:S(2)}, u32[]{:S(2)}) collective-permute-start(f32[8,128]{1,0:T(8,128)S(1)} %slice.13), channel_id=1, source_target_pairs={{0,4},{1,5},{2,6},{3,7},{8,12},{9,13},{10,14},{11,15},{16,20},{17,... | collective-permute-start | bytes 12296 | tf_op jit(solution)/shard_map/ppermute | solution.py:291
  131.3 0.0 collective-permute-done.14.refs_12_
  131.4 10.6 %shard_map.46.late = f32[1024,256]{1,0:T(8,128)} custom-call(f32[4,1024,256]{2,1,0:T(8,128)} %collective-permute-done.6.refs_4_.refs_5_.refs_0_.refs_1_.refs_2_.refs_3_, f32[4,1024,256]{2,1,0:T(8,128)} %collective-permute-done.6.refs_4_.refs_5_.refs_0_.refs_1_.refs_2_.refs_3_, ...), custom_call_target="tpu_custom_call" | custom-call | flops 4831838208 | bytes 14680064 | tf_op jit(solution)/shard_map/pallas_call | solution.py:57
  142.0 0.0 collective-permute-done.17.token
  142.0 0.6 copy-done.4
  142.6 2.7 %shard_map.48 = (f32[1024,256]{1,0:T(8,128)}, f32[1,256]{1,0:T(1,128)}) custom-call(f32[1024,256]{1,0:T(8,128)} %shard_map.46.late, f32[4,1024,256]{2,1,0:T(8,128)} %shard_map.41.whole, f32[1024,256]{1,0:T(8,128)} %collective-permute-done.16.early, f32[1,1024]{1,0:T(1,128)} %bitcast.6, f32[8,128]{1,0:T(8,128)} %copy-done.4), custom_call_target="tpu_custom_call" | custom-call | flops 1048576 | bytes 4194304 | tf_op jit(solution)/shard_map/pallas_call | solution.py:57
  (15 shorter events, 0.0 us)
Async XLA Ops:
  1.9 26.6 %collective-permute-start.1 = (f32[1024,256]{1,0:T(8,128)S(1)}, f32[1024,256]{1,0:T(8,128)S(1)}, u32[]{:S(2)}, u32[]{:S(2)}) collective-permute-start(f32[1024,256]{1,0:T(8,128)S(1)} %slice_bitcast_fusion.1), channel_id=1, source_target_pairs={{0,1},{1,2},{2,3},{3,0},{4,12},{5,13},{6,14},{7,15},{8,9},{9,10},{... | collective-permute-start | bytes 3145736 | tf_op jit(solution)/shard_map/ppermute | solution.py:291
  7.3 22.0 %collective-permute-start.3 = (f32[1024,256]{1,0:T(8,128)S(1)}, f32[1024,256]{1,0:T(8,128)S(1)}, u32[]{:S(2)}, u32[]{:S(2)}) collective-permute-start(f32[1024,256]{1,0:T(8,128)S(1)} %slice_bitcast_fusion), channel_id=1, source_target_pairs={{0,3},{1,0},{2,1},{3,2},{8,11},{9,8},{10,9},{11,10},{16,19},{17,16... | collective-permute-start | bytes 3145736 | tf_op jit(solution)/shard_map/ppermute | solution.py:291
  8.0 31.8 %collective-permute-start.5 = (f32[1024,256]{1,0:T(8,128)S(1)}, f32[1024,256]{1,0:T(8,128)}, u32[]{:S(2)}, u32[]{:S(2)}) collective-permute-start(f32[1024,256]{1,0:T(8,128)S(1)} %slice_bitcast_fusion), channel_id=1, source_target_pairs={{0,1},{1,2},{2,3},{3,0},{4,12},{5,13},{6,14},{7,15},{8,9},{9,10},{... | collective-permute-start | bytes 3145736 | tf_op jit(solution)/shard_map/ppermute | solution.py:291
  11.2 28.6 %collective-permute-start = (f32[1024,256]{1,0:T(8,128)S(1)}, f32[1024,256]{1,0:T(8,128)S(1)}, u32[]{:S(2)}, u32[]{:S(2)}) collective-permute-start(f32[1024,256]{1,0:T(8,128)S(1)} %slice_bitcast_fusion.1), channel_id=1, source_target_pairs={{0,3},{1,0},{2,1},{3,2},{8,11},{9,8},{10,9},{11,10},{16,19},{17,16... | collective-permute-start | bytes 3145736 | tf_op jit(solution)/shard_map/ppermute | solution.py:291
  28.5 11.3 %copy-start.3 = (f32[1024,256]{1,0:T(8,128)}, f32[1024,256]{1,0:T(8,128)S(1)}, u32[]{:S(2)}) copy-start(f32[1024,256]{1,0:T(8,128)S(1)} %collective-permute-done.1.refs_3_.refs_0_) | copy-start | bytes 3145732
  28.5 11.4 %collective-permute-start.2 = (f32[1024,256]{1,0:T(8,128)S(1)}, f32[1024,256]{1,0:T(8,128)S(1)}, u32[]{:S(2)}, u32[]{:S(2)}) collective-permute-start(f32[1024,256]{1,0:T(8,128)S(1)} %collective-permute-done.1.refs_3_.refs_0_), channel_id=1, source_target_pairs={{0,1},{1,2},{2,3},{3,0},{8,9},{9,10},{10,11},{11,8},{16,17},{17,18... | collective-permute-start | bytes 3145736 | tf_op jit(solution)/shard_map/ppermute | solution.py:291
  29.2 10.6 %copy-start.5 = (f32[1024,256]{1,0:T(8,128)}, f32[1024,256]{1,0:T(8,128)S(1)}, u32[]{:S(2)}) copy-start(f32[1024,256]{1,0:T(8,128)S(1)} %collective-permute-done.3.refs_5_) | copy-start | bytes 3145732
  29.2 12.6 %collective-permute-start.4 = (f32[1024,256]{1,0:T(8,128)S(1)}, f32[1024,256]{1,0:T(8,128)}, u32[]{:S(2)}, u32[]{:S(2)}) collective-permute-start(f32[1024,256]{1,0:T(8,128)S(1)} %collective-permute-done.3.refs_5_), channel_id=1, source_target_pairs={{0,3},{1,0},{2,1},{3,2},{8,11},{9,8},{10,9},{11,10},{16,19},{17,16... | collective-permute-start | bytes 3145736 | tf_op jit(solution)/shard_map/ppermute | solution.py:291
  39.8 1.0 copy-start.6
  40.8 1.0 copy-start.7
  44.1 28.4 %collective-permute-start.6 = (f32[4,1024,256]{2,1,0:T(8,128)}, f32[4,1024,256]{2,1,0:T(8,128)}, u32[]{:S(2)}, u32[]{:S(2)}) collective-permute-start(f32[4,1024,256]{2,1,0:T(8,128)} %shard_map.41.whole), channel_id=1, source_target_pairs={{0,4},{1,5},{2,6},{3,7},{8,12},{9,13},{10,14},{11,15},{16,20},{17,... | collective-permute-start | bytes 12582920 | tf_op jit(solution)/shard_map/ppermute | solution.py:291
  45.4 8.5 %collective-permute-start.11 = (f32[1024,256]{1,0:T(8,128)}, f32[1024,256]{1,0:T(8,128)S(1)}, u32[]{:S(2)}, u32[]{:S(2)}) collective-permute-start(f32[1024,256]{1,0:T(8,128)} %collective-permute-done.5.refs_7_.refs_0_.refs_3_), channel_id=1, source_target_pairs={{12,13},{13,14},{14,15},{15,12},{20,21},{21,22},{22,23},{23,20},{2... | collective-permute-start | bytes 3145736 | tf_op jit(solution)/shard_map/ppermute | solution.py:291
  46.1 9.6 %collective-permute-start.10 = (f32[1024,256]{1,0:T(8,128)}, f32[1024,256]{1,0:T(8,128)S(1)}, u32[]{:S(2)}, u32[]{:S(2)}) collective-permute-start(f32[1024,256]{1,0:T(8,128)} %collective-permute-done.5.refs_7_.refs_0_.refs_3_), channel_id=1, source_target_pairs={{12,15},{13,12},{14,13},{15,14},{20,23},{21,20},{22,21},{23,22},{2... | collective-permute-start | bytes 3145736 | tf_op jit(solution)/shard_map/ppermute | solution.py:291
  46.8 16.4 %collective-permute-start.7 = (f32[1024,256]{1,0:T(8,128)}, f32[1024,256]{1,0:T(8,128)}, u32[]{:S(2)}, u32[]{:S(2)}) collective-permute-start(f32[1024,256]{1,0:T(8,128)} %copy-done.3), channel_id=1, source_target_pairs={{4,7},{5,4},{6,5},{7,6},{12,15},{13,12},{14,13},{15,14},{20,23},{2... | collective-permute-start | bytes 3145736 | tf_op jit(solution)/shard_map/ppermute | solution.py:291
  51.2 80.1 %collective-permute-start.13 = (f32[4,1024,256]{2,1,0:T(8,128)}, f32[4,1024,256]{2,1,0:T(8,128)}, u32[]{:S(2)}, u32[]{:S(2)}) collective-permute-start(f32[4,1024,256]{2,1,0:T(8,128)} %shard_map.41.whole), channel_id=1, source_target_pairs={{0,12},{1,13},{2,14},{3,15},{8,20},{9,21},{10,22},{11,23},{16,28},... | collective-permute-start | bytes 12582920 | tf_op jit(solution)/shard_map/ppermute | solution.py:291
  53.9 1.1 copy-start
  54.9 13.3 %collective-permute-start.12 = (f32[1024,256]{1,0:T(8,128)S(1)}, f32[1024,256]{1,0:T(8,128)S(1)}, u32[]{:S(2)}, u32[]{:S(2)}) collective-permute-start(f32[1024,256]{1,0:T(8,128)S(1)} %collective-permute-done.11.refs_3_.refs_6_), channel_id=1, source_target_pairs={{12,13},{13,14},{14,15},{15,12},{20,21},{21,22},{22,23},{23,20},{2... | collective-permute-start | bytes 3145736 | tf_op jit(solution)/shard_map/ppermute | solution.py:291
  55.7 12.6 %copy-start.1 = (f32[1024,256]{1,0:T(8,128)}, f32[1024,256]{1,0:T(8,128)S(1)}, u32[]{:S(2)}) copy-start(f32[1024,256]{1,0:T(8,128)S(1)} %collective-permute-done.10.refs_1_.refs_4_) | copy-start | bytes 3145732
  55.7 26.8 %collective-permute-start.9 = (f32[1024,256]{1,0:T(8,128)}, f32[1024,256]{1,0:T(8,128)}, u32[]{:S(2)}, u32[]{:S(2)}) collective-permute-start(f32[1024,256]{1,0:T(8,128)} %copy-done.3), channel_id=1, source_target_pairs={{4,5},{5,6},{6,7},{7,4},{12,13},{13,14},{14,15},{15,12},{20,21},{2... | collective-permute-start | bytes 3145736 | tf_op jit(solution)/shard_map/ppermute | solution.py:291
  63.3 19.2 %collective-permute-start.8 = (f32[1024,256]{1,0:T(8,128)}, f32[1024,256]{1,0:T(8,128)}, u32[]{:S(2)}, u32[]{:S(2)}) collective-permute-start(f32[1024,256]{1,0:T(8,128)} %collective-permute-done.7.refs_1_), channel_id=1, source_target_pairs={{4,7},{5,4},{6,5},{7,6},{12,15},{13,12},{14,13},{15,14},{20,23},{2... | collective-permute-start | bytes 3145736 | tf_op jit(solution)/shard_map/ppermute | solution.py:291
  68.3 1.0 copy-start.2
  88.0 31.1 %collective-permute-start.15 = (f32[1024,256]{1,0:T(8,128)}, f32[1024,256]{1,0:T(8,128)}, u32[]{:S(2)}, u32[]{:S(2)}) collective-permute-start(f32[1024,256]{1,0:T(8,128)} %get-tuple-element.7), channel_id=1, source_target_pairs={{12,4},{13,5},{14,6},{15,7},{20,12},{21,13},{22,14},{23,15},{28,20... | collective-permute-start | bytes 3145736 | tf_op jit(solution)/shard_map/ppermute | solution.py:291
  89.3 42.1 %collective-permute-start.14 = (f32[1024,256]{1,0:T(8,128)}, f32[1024,256]{1,0:T(8,128)}, u32[]{:S(2)}, u32[]{:S(2)}) collective-permute-start(f32[1024,256]{1,0:T(8,128)} %get-tuple-element.6.refs_4_), channel_id=1, source_target_pairs={{4,508},{5,509},{6,510},{7,511},{12,4},{13,5},{14,6},{15,7},{20,12... | collective-permute-start | bytes 3145736 | tf_op jit(solution)/shard_map/ppermute | solution.py:291
  126.9 15.1 %collective-permute-start.16 = (f32[1024,256]{1,0:T(8,128)}, f32[1024,256]{1,0:T(8,128)}, u32[]{:S(2)}, u32[]{:S(2)}) collective-permute-start(f32[1024,256]{1,0:T(8,128)} %shard_map.47), channel_id=1, source_target_pairs={{4,8},{5,9},{6,10},{7,11},{12,16},{13,17},{14,18},{15,19},{20,24},... | collective-permute-start | bytes 3145736 | tf_op jit(solution)/shard_map/ppermute | solution.py:291
  129.9 12.1 %collective-permute-start.17 = (f32[8,128]{1,0:T(8,128)S(1)}, f32[8,128]{1,0:T(8,128)S(1)}, u32[]{:S(2)}, u32[]{:S(2)}) collective-permute-start(f32[8,128]{1,0:T(8,128)S(1)} %slice.13), channel_id=1, source_target_pairs={{0,4},{1,5},{2,6},{3,7},{8,12},{9,13},{10,14},{11,15},{16,20},{17,... | collective-permute-start | bytes 12296 | tf_op jit(solution)/shard_map/ppermute | solution.py:291
  142.0 0.6 copy-start.4

commit v3 on v2

--- a/solution.py
+++ b/solution.py
@@ -70,13 +70,13 @@
     return lambda i: jnp.where(place()[1] == on, index(i), 0)
 
 
-def product_kernel(n_left, picks, width, on, *refs):
+def product_kernel(n_left, picks, width, on, since, *refs):
     n_right = len(picks)
     lefts, rights, (out, held, v, sems) = refs[:n_left], refs[n_left : n_left + n_right], refs[n_left + n_right :]
     i = pl.program_id(0)
-    _, core, x = place()
-
-    @pl.when(core == on)
+    k, core, x = place()
+
+    @pl.when((core == on) & (k >= since))
     def _():
         @pl.when(i == 0)
         def _():
@@ -94,13 +94,13 @@
             out[j] = total[:, j * width : (j + 1) * width]
 
 
-def product(left, right, on):
+def product(left, right, on, since=0):
     rows, depth = left[0][0].shape[-2:]
     width = right[0][0].shape[-1]
     n, full = len(right), len(left) * depth
     step = only(on, lambda i: i)
     return call_kernel(
-        functools.partial(product_kernel, len(left), [p[1] for p in right], width, on),
+        functools.partial(product_kernel, len(left), [p[1] for p in right], width, on, since),
         jax.ShapeDtypeStruct((n, rows, width), jnp.float32),
         rows // TILE,
         [spec(p, TILE, step) for p in left] + [pl.BlockSpec(memory_space=pl.ANY)] * n,
@@ -116,7 +116,7 @@
     )
 
 
-def chain_kernel(counts, tiles, on, passes, *refs):
+def chain_kernel(counts, tiles, on, since, passes, *refs):
     n_left = sum(counts)
     lefts, (right, out, v) = refs[:n_left], refs[n_left:]
     i = pl.program_id(0)
@@ -124,7 +124,7 @@
     depth = lefts[0].shape[1]
     blocks = CHAIN_TILE // depth
     tile = lax.rem(i, tiles)
-    active = core == on
+    active = (core == on) & (k >= since)
 
     @pl.when(active & (i == 0))
     def _():
@@ -159,7 +159,7 @@
                     put(v.at[later], x, tile * blocks + h, slice(None), high + low)
 
 
-def chain(lefts, right, on, passes):
+def chain(lefts, right, on, passes, since=0):
     rows, _ = lefts[0][0][0].shape[-2:]
     width = right[0].shape[-1]
     tiles, n = rows // CHAIN_TILE, len(lefts)
@@ -167,7 +167,7 @@
     for m, left in enumerate(lefts):
         specs += [spec(p, CHAIN_TILE, only(on, lambda i, m=m: jnp.clip(i - m * tiles, 0, tiles - 1))) for p in left]
     return call_kernel(
-        functools.partial(chain_kernel, [len(left) for left in lefts], tiles, on, passes),
+        functools.partial(chain_kernel, [len(left) for left in lefts], tiles, on, since, passes),
         jax.ShapeDtypeStruct((rows, width), jnp.float32),
         n * tiles,
         specs + [spec(right, rows, lambda i: 0)],
@@ -321,14 +321,14 @@
     left = panels((a_odd, None), a_odd_right, a_odd_far, a_odd_left)
     right = panels((c_odd, None), c_odd_right, c_odd_far, c_odd_left)
     here = even_here[0]
-    inner = chain([right], here, 1, (False,))
+    inner = chain([right], here, 1, (False,), since=1)
     pairs = [(inner, None), right[0]]
     begun = pair({0: left[0], 1: left[1]}, pairs)
     step, ahead = pair({2: left[2], 3: left[3]}, pairs, begun, here)
     there = send(step, None, (-1, 1, 0))
     own = ahead
     ahead = send(ahead, None, (-1, 1, 0), wrap=True)
-    rest = product(left, right[1:], 1)
+    rest = product(left, right[1:], 1, since=1)
     odd = [(own, None)] + [(rest, j) for j in range(n_x - 1)]
     step = chain([even_here, odd], (there, None), 1, (False, True))
     early = send(step, None, (1, 0, 0))

time: 146 us -> 140 us (0.959)
  Pallas kernels: 49.2 us -> 41.5 us
  starting transfers between devices: 53.1 us -> 54.7 us
    pallas_call x8, Pallas kernels: 49.2 us -> 41.5 us  [call_kernel(): pl.pallas_call(kernel, out_shape=out_shape, grid=(grid,), in_specs=specs,...]
    ppermute x18, starting transfers between devices: 53.1 us -> 54.7 us  [send(): return lax.ppermute(a, ('tm', 'panel'), pairs)]
  transfers between devices with their start and end apart: 18 -> 18, of which waited for: 4 -> 4; matrix products, arithmetic and copies ran while one was open for 1% -> 1% of each run, Pallas kernels for 30% -> 26%
where the time goes in v3:
time: 140 us; the launch traced here: 139 us
  starting transfers between devices  54.7 us (39%)
  Pallas kernels  41.5 us (30%)
  waiting for transfers between devices  34.4 us (25%)
  local copies, waits for them, and re-layouts  7.84 us (6%)
    ppermute x18, starting transfers between devices, send(): return lax.ppermute(a, ('tm', 'panel'), pairs)  54.7 us
    pallas_call x8, Pallas kernels, call_kernel(): pl.pallas_call(kernel, out_shape=out_shape, grid=(grid,), in_specs=specs,...  41.5 us
    ppermute x18, waiting for transfers between devices, send(): return lax.ppermute(a, ('tm', 'panel'), pairs)  34.4 us
    unnamed x16, local copies, waits for them, and re-layouts  4.57 us
  transfers between devices with their start and end apart: 18, of which 4 were waited for; matrix products, arithmetic and copies ran while one was open for 1% of the time, Pallas kernels for 26%

profile of v3, /device:TPU:1, one launch (start us, length us, event | category | flops | bytes accessed | tf_op | source)
XLA Modules:
  0.0 139.4 jit_solution(6369153366475054464)
XLA Ops:
  0.6 1.3 slice_bitcast_fusion.1
  1.9 4.0 %collective-permute-start.1 = (f32[1024,256]{1,0:T(8,128)S(1)}, f32[1024,256]{1,0:T(8,128)S(1)}, u32[]{:S(2)}, u32[]{:S(2)}) collective-permute-start(f32[1024,256]{1,0:T(8,128)S(1)} %slice_bitcast_fusion.1), channel_id=1, source_target_pairs={{0,1},{1,2},{2,3},{3,0},{4,12},{5,13},{6,14},{7,15},{8,9},{9,10},{... | collective-permute-start | bytes 3145736 | tf_op jit(solution)/shard_map/ppermute | solution.py:291
  6.0 1.3 slice_bitcast_fusion
  7.3 0.7 collective-permute-start.3
  8.0 3.2 %collective-permute-start.5 = (f32[1024,256]{1,0:T(8,128)S(1)}, f32[1024,256]{1,0:T(8,128)}, u32[]{:S(2)}, u32[]{:S(2)}) collective-permute-start(f32[1024,256]{1,0:T(8,128)S(1)} %slice_bitcast_fusion), channel_id=1, source_target_pairs={{0,1},{1,2},{2,3},{3,0},{4,12},{5,13},{6,14},{7,15},{8,9},{9,10},{... | collective-permute-start | bytes 3145736 | tf_op jit(solution)/shard_map/ppermute | solution.py:291
  11.2 0.7 collective-permute-start
  11.9 16.6 %collective-permute-done.1.refs_3_.refs_0_ = f32[1024,256]{1,0:T(8,128)S(1)} collective-permute-done((f32[1024,256]{1,0:T(8,128)S(1)}, f32[1024,256]{1,0:T(8,128)S(1)}, u32[]{:S(2)}, u32[]{:S(2)}) %collective-permute-start.1) | collective-permute-done | bytes 1048608 | tf_op jit(solution)/shard_map/ppermute | solution.py:291
  28.5 0.7 collective-permute-start.2
  29.2 0.0 collective-permute-done.3.refs_5_
  29.2 1.6 %collective-permute-start.4 = (f32[1024,256]{1,0:T(8,128)S(1)}, f32[1024,256]{1,0:T(8,128)}, u32[]{:S(2)}, u32[]{:S(2)}) collective-permute-start(f32[1024,256]{1,0:T(8,128)S(1)} %collective-permute-done.3.refs_5_), channel_id=1, source_target_pairs={{0,3},{1,0},{2,1},{3,2},{8,11},{9,8},{10,9},{11,10},{16,19},{17,16... | collective-permute-start | bytes 3145736 | tf_op jit(solution)/shard_map/ppermute | solution.py:291
  30.9 9.0 %collective-permute-done.5.refs_7_.refs_0_.refs_3_ = f32[1024,256]{1,0:T(8,128)} collective-permute-done((f32[1024,256]{1,0:T(8,128)S(1)}, f32[1024,256]{1,0:T(8,128)}, u32[]{:S(2)}, u32[]{:S(2)}) %collective-permute-start.5) | collective-permute-done | bytes 1048608 | tf_op jit(solution)/shard_map/ppermute | solution.py:291
  39.8 0.0 collective-permute-done.refs_1_
  39.9 0.0 collective-permute-done.2.refs_2_
  39.9 0.9 copy-done.6
  40.8 1.0 copy-done.7
  41.8 0.0 collective-permute-done.4.refs_6_
  41.8 2.2 %shard_map.41.whole = f32[4,1024,256]{2,1,0:T(8,128)} custom-call(f32[2,1024,256]{2,1,0:T(8,128)} %refs_4_.1, f32[1024,256]{1,0:T(8,128)} %copy-done.6, f32[1024,256]{1,0:T(8,128)} %copy-done.7, f32[1024,256]{1,0:T(8,128)} %copy-done.3, f32[2,1024,256]{2,1,0:T(8,128)} %refs_4_.1, f32[1024,256]{1,0:T(8,128)} %copy-done.5, ...), custom_call_target="tpu_custom_call" | custom-call | flops 6442450944 | bytes 12582912 | tf_op jit(solution)/shard_map/pallas_call | solution.py:57
  44.1 1.3 collective-permute-start.6
  45.4 0.7 collective-permute-start.11
  46.1 0.7 collective-permute-start.10
  46.8 4.4 %collective-permute-start.7 = (f32[1024,256]{1,0:T(8,128)}, f32[1024,256]{1,0:T(8,128)}, u32[]{:S(2)}, u32[]{:S(2)}) collective-permute-start(f32[1024,256]{1,0:T(8,128)} %copy-done.3), channel_id=1, source_target_pairs={{4,7},{5,4},{6,5},{7,6},{12,15},{13,12},{14,13},{15,14},{20,23},{2... | collective-permute-start | bytes 3145736 | tf_op jit(solution)/shard_map/ppermute | solution.py:291
  51.2 2.6 %collective-permute-start.13 = (f32[4,1024,256]{2,1,0:T(8,128)}, f32[4,1024,256]{2,1,0:T(8,128)}, u32[]{:S(2)}, u32[]{:S(2)}) collective-permute-start(f32[4,1024,256]{2,1,0:T(8,128)} %shard_map.41.whole), channel_id=1, source_target_pairs={{0,12},{1,13},{2,14},{3,15},{8,20},{9,21},{10,22},{11,23},{16,28},... | collective-permute-start | bytes 12582920 | tf_op jit(solution)/shard_map/ppermute | solution.py:291
  53.9 0.0 collective-permute-done.11.refs_3_.refs_6_
  53.9 1.1 copy-done
  54.9 0.7 collective-permute-start.12
  55.7 0.0 collective-permute-done.10.refs_1_.refs_4_
  55.7 0.0 copy-start.1
  55.7 1.9 %collective-permute-start.9 = (f32[1024,256]{1,0:T(8,128)}, f32[1024,256]{1,0:T(8,128)}, u32[]{:S(2)}, u32[]{:S(2)}) collective-permute-start(f32[1024,256]{1,0:T(8,128)} %copy-done.3), channel_id=1, source_target_pairs={{4,5},{5,6},{6,7},{7,4},{12,13},{13,14},{14,15},{15,12},{20,21},{2... | collective-permute-start | bytes 3145736 | tf_op jit(solution)/shard_map/ppermute | solution.py:291
  57.6 5.6 %collective-permute-done.7.refs_1_ = f32[1024,256]{1,0:T(8,128)} collective-permute-done((f32[1024,256]{1,0:T(8,128)}, f32[1024,256]{1,0:T(8,128)}, u32[]{:S(2)}, u32[]{:S(2)}) %collective-permute-start.7) | collective-permute-done | bytes 1048608 | tf_op jit(solution)/shard_map/ppermute | solution.py:291
  63.3 5.0 %collective-permute-start.8 = (f32[1024,256]{1,0:T(8,128)}, f32[1024,256]{1,0:T(8,128)}, u32[]{:S(2)}, u32[]{:S(2)}) collective-permute-start(f32[1024,256]{1,0:T(8,128)} %collective-permute-done.7.refs_1_), channel_id=1, source_target_pairs={{4,7},{5,4},{6,5},{7,6},{12,15},{13,12},{14,13},{15,14},{20,23},{2... | collective-permute-start | bytes 3145736 | tf_op jit(solution)/shard_map/ppermute | solution.py:291
  68.3 0.0 collective-permute-done.12.refs_2_.refs_5_
  68.3 1.0 copy-done.2
  69.3 3.2 %collective-permute-done.6.refs_4_.refs_5_.refs_0_.refs_1_.refs_2_.refs_3_ = f32[4,1024,256]{2,1,0:T(8,128)} collective-permute-done((f32[4,1024,256]{2,1,0:T(8,128)}, f32[4,1024,256]{2,1,0:T(8,128)}, u32[]{:S(2)}, u32[]{:S(2)}) %collective-permute-start.6) | collective-permute-done | bytes 4194336 | tf_op jit(solution)/shard_map/ppermute | solution.py:291
  72.5 3.3 %shard_map.42.refs_2_ = f32[1024,256]{1,0:T(8,128)} custom-call(f32[1024,256]{1,0:T(8,128)} %collective-permute-done.5.refs_7_.refs_0_.refs_3_, f32[1024,256]{1,0:T(8,128)} %copy-done.1, f32[1024,256]{1,0:T(8,128)} %copy-done.2, f32[1024,256]{1,0:T(8,128)} %copy-done, f32[4,1024,256]{2,1,0:T(8,128)} %collective-permute-done.6.refs_4_.refs_5_.refs_0_.refs_1_.refs_2_.refs_3_), custom_call_target="tpu_custom_call" | custom-call | flops 1610612736 | bytes 6291456 | tf_op jit(solution)/shard_map/pallas_call | solution.py:57
  75.7 5.0 %shard_map.43.refs_4_ = f32[2,1024,256]{2,1,0:T(8,128)} custom-call(f32[1024,256]{1,0:T(8,128)} %copy-done.3, f32[1024,256]{1,0:T(8,128)} %collective-permute-done.7.refs_1_, f32[1024,256]{1,0:T(8,128)} %shard_map.42.refs_2_, f32[1024,256]{1,0:T(8,128)} %collective-permute-done.5.refs_7_.refs_0_.refs_3_), custom_call_target="tpu_custom_call" | custom-call | flops 1610612736 | bytes 8388608 | tf_op jit(solution)/shard_map/pallas_call | solution.py:57
  80.8 5.5 %shard_map.44 = (f32[1024,256]{1,0:T(8,128)}, f32[1024,256]{1,0:T(8,128)}) custom-call(f32[1024,256]{1,0:T(8,128)} %collective-permute-done.8.refs_0_.refs_2_, f32[1024,256]{1,0:T(8,128)} %collective-permute-done.9.refs_1_.refs_3_, f32[1024,256]{1,0:T(8,128)} %shard_map.42.refs_2_, f32[1024,256]{1,0:T(8,128)} %collective-permute-done.5.refs_7_.refs_0_.refs_3_, ...), custom_call_target="tpu_custom_call" | custom-call | flops 1610612736 | bytes 8388608 | tf_op jit(solution)/shard_map/pallas_call | solution.py:57
  86.3 1.3 collective-permute-start.15
  87.6 21.2 %collective-permute-start.14 = (f32[1024,256]{1,0:T(8,128)}, f32[1024,256]{1,0:T(8,128)}, u32[]{:S(2)}, u32[]{:S(2)}) collective-permute-start(f32[1024,256]{1,0:T(8,128)} %get-tuple-element.6.refs_4_), channel_id=1, source_target_pairs={{4,508},{5,509},{6,510},{7,511},{12,4},{13,5},{14,6},{15,7},{20,12... | collective-permute-start | bytes 3145736 | tf_op jit(solution)/shard_map/ppermute | solution.py:291
  108.8 4.3 %shard_map.45.refs_5_.refs_6_.refs_7_ = f32[3,1024,256]{2,1,0:T(8,128)} custom-call(f32[1024,256]{1,0:T(8,128)} %copy-done.3, f32[1024,256]{1,0:T(8,128)} %collective-permute-done.7.refs_1_, f32[1024,256]{1,0:T(8,128)} %collective-permute-done.8.refs_0_.refs_2_, f32[1024,256]{1,0:T(8,128)} %collective-permute-done.9.refs_1_.refs_3_, f32[1024,256]{1,0:T(8,128)} %copy-done.1, ...), custom_call_target="tpu_custom_call" | custom-call | flops 4831838208 | bytes 10485760 | tf_op jit(solution)/shard_map/pallas_call | solution.py:57
  113.1 7.8 %shard_map.47 = f32[1024,256]{1,0:T(8,128)} custom-call(f32[4,1024,256]{2,1,0:T(8,128)} %collective-permute-done.6.refs_4_.refs_5_.refs_0_.refs_1_.refs_2_.refs_3_, f32[4,1024,256]{2,1,0:T(8,128)} %collective-permute-done.6.refs_4_.refs_5_.refs_0_.refs_1_.refs_2_.refs_3_, ...), custom_call_target="tpu_custom_call" | custom-call | flops 3221225472 | bytes 10485760 | tf_op jit(solution)/shard_map/pallas_call | solution.py:57
  120.9 2.3 %collective-permute-start.16 = (f32[1024,256]{1,0:T(8,128)}, f32[1024,256]{1,0:T(8,128)}, u32[]{:S(2)}, u32[]{:S(2)}) collective-permute-start(f32[1024,256]{1,0:T(8,128)} %shard_map.47), channel_id=1, source_target_pairs={{4,8},{5,9},{6,10},{7,11},{12,16},{13,17},{14,18},{15,19},{20,24},... | collective-permute-start | bytes 3145736 | tf_op jit(solution)/shard_map/ppermute | solution.py:291
  123.2 0.7 slice.13
  123.9 1.5 %collective-permute-start.17 = (f32[8,128]{1,0:T(8,128)S(1)}, f32[8,128]{1,0:T(8,128)S(1)}, u32[]{:S(2)}, u32[]{:S(2)}) collective-permute-start(f32[8,128]{1,0:T(8,128)S(1)} %slice.13), channel_id=1, source_target_pairs={{0,4},{1,5},{2,6},{3,7},{8,12},{9,13},{10,14},{11,15},{16,20},{17,... | collective-permute-start | bytes 12296 | tf_op jit(solution)/shard_map/ppermute | solution.py:291
  125.4 0.0 collective-permute-done.13.refs_8_.refs_9_.refs_10_.refs_11_
  125.4 10.7 %shard_map.46.late = f32[1024,256]{1,0:T(8,128)} custom-call(f32[4,1024,256]{2,1,0:T(8,128)} %collective-permute-done.6.refs_4_.refs_5_.refs_0_.refs_1_.refs_2_.refs_3_, f32[4,1024,256]{2,1,0:T(8,128)} %collective-permute-done.6.refs_4_.refs_5_.refs_0_.refs_1_.refs_2_.refs_3_, ...), custom_call_target="tpu_custom_call" | custom-call | flops 4831838208 | bytes 14680064 | tf_op jit(solution)/shard_map/pallas_call | solution.py:57
  136.1 0.0 collective-permute-done.17.token
  136.1 0.6 copy-done.4
  136.7 2.7 %shard_map.48 = (f32[1024,256]{1,0:T(8,128)}, f32[1,256]{1,0:T(1,128)}) custom-call(f32[1024,256]{1,0:T(8,128)} %shard_map.46.late, f32[4,1024,256]{2,1,0:T(8,128)} %shard_map.41.whole, f32[1024,256]{1,0:T(8,128)} %collective-permute-done.16.early, f32[1,1024]{1,0:T(1,128)} %bitcast.6, f32[8,128]{1,0:T(8,128)} %copy-done.4), custom_call_target="tpu_custom_call" | custom-call | flops 1048576 | bytes 4194304 | tf_op jit(solution)/shard_map/pallas_call | solution.py:57
  (15 shorter events, 0.0 us)
Async XLA Ops:
  1.9 26.6 %collective-permute-start.1 = (f32[1024,256]{1,0:T(8,128)S(1)}, f32[1024,256]{1,0:T(8,128)S(1)}, u32[]{:S(2)}, u32[]{:S(2)}) collective-permute-start(f32[1024,256]{1,0:T(8,128)S(1)} %slice_bitcast_fusion.1), channel_id=1, source_target_pairs={{0,1},{1,2},{2,3},{3,0},{4,12},{5,13},{6,14},{7,15},{8,9},{9,10},{... | collective-permute-start | bytes 3145736 | tf_op jit(solution)/shard_map/ppermute | solution.py:291
  7.3 22.0 %collective-permute-start.3 = (f32[1024,256]{1,0:T(8,128)S(1)}, f32[1024,256]{1,0:T(8,128)S(1)}, u32[]{:S(2)}, u32[]{:S(2)}) collective-permute-start(f32[1024,256]{1,0:T(8,128)S(1)} %slice_bitcast_fusion), channel_id=1, source_target_pairs={{0,3},{1,0},{2,1},{3,2},{8,11},{9,8},{10,9},{11,10},{16,19},{17,16... | collective-permute-start | bytes 3145736 | tf_op jit(solution)/shard_map/ppermute | solution.py:291
  8.0 31.8 %collective-permute-start.5 = (f32[1024,256]{1,0:T(8,128)S(1)}, f32[1024,256]{1,0:T(8,128)}, u32[]{:S(2)}, u32[]{:S(2)}) collective-permute-start(f32[1024,256]{1,0:T(8,128)S(1)} %slice_bitcast_fusion), channel_id=1, source_target_pairs={{0,1},{1,2},{2,3},{3,0},{4,12},{5,13},{6,14},{7,15},{8,9},{9,10},{... | collective-permute-start | bytes 3145736 | tf_op jit(solution)/shard_map/ppermute | solution.py:291
  11.2 28.6 %collective-permute-start = (f32[1024,256]{1,0:T(8,128)S(1)}, f32[1024,256]{1,0:T(8,128)S(1)}, u32[]{:S(2)}, u32[]{:S(2)}) collective-permute-start(f32[1024,256]{1,0:T(8,128)S(1)} %slice_bitcast_fusion.1), channel_id=1, source_target_pairs={{0,3},{1,0},{2,1},{3,2},{8,11},{9,8},{10,9},{11,10},{16,19},{17,16... | collective-permute-start | bytes 3145736 | tf_op jit(solution)/shard_map/ppermute | solution.py:291
  28.5 11.3 %copy-start.3 = (f32[1024,256]{1,0:T(8,128)}, f32[1024,256]{1,0:T(8,128)S(1)}, u32[]{:S(2)}) copy-start(f32[1024,256]{1,0:T(8,128)S(1)} %collective-permute-done.1.refs_3_.refs_0_) | copy-start | bytes 3145732
  28.5 11.4 %collective-permute-start.2 = (f32[1024,256]{1,0:T(8,128)S(1)}, f32[1024,256]{1,0:T(8,128)S(1)}, u32[]{:S(2)}, u32[]{:S(2)}) collective-permute-start(f32[1024,256]{1,0:T(8,128)S(1)} %collective-permute-done.1.refs_3_.refs_0_), channel_id=1, source_target_pairs={{0,1},{1,2},{2,3},{3,0},{8,9},{9,10},{10,11},{11,8},{16,17},{17,18... | collective-permute-start | bytes 3145736 | tf_op jit(solution)/shard_map/ppermute | solution.py:291
  29.2 10.6 %copy-start.5 = (f32[1024,256]{1,0:T(8,128)}, f32[1024,256]{1,0:T(8,128)S(1)}, u32[]{:S(2)}) copy-start(f32[1024,256]{1,0:T(8,128)S(1)} %collective-permute-done.3.refs_5_) | copy-start | bytes 3145732
  29.2 12.6 %collective-permute-start.4 = (f32[1024,256]{1,0:T(8,128)S(1)}, f32[1024,256]{1,0:T(8,128)}, u32[]{:S(2)}, u32[]{:S(2)}) collective-permute-start(f32[1024,256]{1,0:T(8,128)S(1)} %collective-permute-done.3.refs_5_), channel_id=1, source_target_pairs={{0,3},{1,0},{2,1},{3,2},{8,11},{9,8},{10,9},{11,10},{16,19},{17,16... | collective-permute-start | bytes 3145736 | tf_op jit(solution)/shard_map/ppermute | solution.py:291
  39.8 1.0 copy-start.6
  40.8 1.0 copy-start.7
  44.1 28.4 %collective-permute-start.6 = (f32[4,1024,256]{2,1,0:T(8,128)}, f32[4,1024,256]{2,1,0:T(8,128)}, u32[]{:S(2)}, u32[]{:S(2)}) collective-permute-start(f32[4,1024,256]{2,1,0:T(8,128)} %shard_map.41.whole), channel_id=1, source_target_pairs={{0,4},{1,5},{2,6},{3,7},{8,12},{9,13},{10,14},{11,15},{16,20},{17,... | collective-permute-start | bytes 12582920 | tf_op jit(solution)/shard_map/ppermute | solution.py:291
  45.4 8.5 %collective-permute-start.11 = (f32[1024,256]{1,0:T(8,128)}, f32[1024,256]{1,0:T(8,128)S(1)}, u32[]{:S(2)}, u32[]{:S(2)}) collective-permute-start(f32[1024,256]{1,0:T(8,128)} %collective-permute-done.5.refs_7_.refs_0_.refs_3_), channel_id=1, source_target_pairs={{12,13},{13,14},{14,15},{15,12},{20,21},{21,22},{22,23},{23,20},{2... | collective-permute-start | bytes 3145736 | tf_op jit(solution)/shard_map/ppermute | solution.py:291
  46.1 9.6 %collective-permute-start.10 = (f32[1024,256]{1,0:T(8,128)}, f32[1024,256]{1,0:T(8,128)S(1)}, u32[]{:S(2)}, u32[]{:S(2)}) collective-permute-start(f32[1024,256]{1,0:T(8,128)} %collective-permute-done.5.refs_7_.refs_0_.refs_3_), channel_id=1, source_target_pairs={{12,15},{13,12},{14,13},{15,14},{20,23},{21,20},{22,21},{23,22},{2... | collective-permute-start | bytes 3145736 | tf_op jit(solution)/shard_map/ppermute | solution.py:291
  46.8 16.4 %collective-permute-start.7 = (f32[1024,256]{1,0:T(8,128)}, f32[1024,256]{1,0:T(8,128)}, u32[]{:S(2)}, u32[]{:S(2)}) collective-permute-start(f32[1024,256]{1,0:T(8,128)} %copy-done.3), channel_id=1, source_target_pairs={{4,7},{5,4},{6,5},{7,6},{12,15},{13,12},{14,13},{15,14},{20,23},{2... | collective-permute-start | bytes 3145736 | tf_op jit(solution)/shard_map/ppermute | solution.py:291
  51.2 74.2 %collective-permute-start.13 = (f32[4,1024,256]{2,1,0:T(8,128)}, f32[4,1024,256]{2,1,0:T(8,128)}, u32[]{:S(2)}, u32[]{:S(2)}) collective-permute-start(f32[4,1024,256]{2,1,0:T(8,128)} %shard_map.41.whole), channel_id=1, source_target_pairs={{0,12},{1,13},{2,14},{3,15},{8,20},{9,21},{10,22},{11,23},{16,28},... | collective-permute-start | bytes 12582920 | tf_op jit(solution)/shard_map/ppermute | solution.py:291
  53.9 1.1 copy-start
  54.9 13.3 %collective-permute-start.12 = (f32[1024,256]{1,0:T(8,128)S(1)}, f32[1024,256]{1,0:T(8,128)S(1)}, u32[]{:S(2)}, u32[]{:S(2)}) collective-permute-start(f32[1024,256]{1,0:T(8,128)S(1)} %collective-permute-done.11.refs_3_.refs_6_), channel_id=1, source_target_pairs={{12,13},{13,14},{14,15},{15,12},{20,21},{21,22},{22,23},{23,20},{2... | collective-permute-start | bytes 3145736 | tf_op jit(solution)/shard_map/ppermute | solution.py:291
  55.7 12.6 %copy-start.1 = (f32[1024,256]{1,0:T(8,128)}, f32[1024,256]{1,0:T(8,128)S(1)}, u32[]{:S(2)}) copy-start(f32[1024,256]{1,0:T(8,128)S(1)} %collective-permute-done.10.refs_1_.refs_4_) | copy-start | bytes 3145732
  55.7 25.1 %collective-permute-start.9 = (f32[1024,256]{1,0:T(8,128)}, f32[1024,256]{1,0:T(8,128)}, u32[]{:S(2)}, u32[]{:S(2)}) collective-permute-start(f32[1024,256]{1,0:T(8,128)} %copy-done.3), channel_id=1, source_target_pairs={{4,5},{5,6},{6,7},{7,4},{12,13},{13,14},{14,15},{15,12},{20,21},{2... | collective-permute-start | bytes 3145736 | tf_op jit(solution)/shard_map/ppermute | solution.py:291
  63.3 17.5 %collective-permute-start.8 = (f32[1024,256]{1,0:T(8,128)}, f32[1024,256]{1,0:T(8,128)}, u32[]{:S(2)}, u32[]{:S(2)}) collective-permute-start(f32[1024,256]{1,0:T(8,128)} %collective-permute-done.7.refs_1_), channel_id=1, source_target_pairs={{4,7},{5,4},{6,5},{7,6},{12,15},{13,12},{14,13},{15,14},{20,23},{2... | collective-permute-start | bytes 3145736 | tf_op jit(solution)/shard_map/ppermute | solution.py:291
  68.3 1.0 copy-start.2
  86.3 26.8 %collective-permute-start.15 = (f32[1024,256]{1,0:T(8,128)}, f32[1024,256]{1,0:T(8,128)}, u32[]{:S(2)}, u32[]{:S(2)}) collective-permute-start(f32[1024,256]{1,0:T(8,128)} %get-tuple-element.7), channel_id=1, source_target_pairs={{12,4},{13,5},{14,6},{15,7},{20,12},{21,13},{22,14},{23,15},{28,20... | collective-permute-start | bytes 3145736 | tf_op jit(solution)/shard_map/ppermute | solution.py:291
  87.6 37.8 %collective-permute-start.14 = (f32[1024,256]{1,0:T(8,128)}, f32[1024,256]{1,0:T(8,128)}, u32[]{:S(2)}, u32[]{:S(2)}) collective-permute-start(f32[1024,256]{1,0:T(8,128)} %get-tuple-element.6.refs_4_), channel_id=1, source_target_pairs={{4,508},{5,509},{6,510},{7,511},{12,4},{13,5},{14,6},{15,7},{20,12... | collective-permute-start | bytes 3145736 | tf_op jit(solution)/shard_map/ppermute | solution.py:291
  120.9 15.1 %collective-permute-start.16 = (f32[1024,256]{1,0:T(8,128)}, f32[1024,256]{1,0:T(8,128)}, u32[]{:S(2)}, u32[]{:S(2)}) collective-permute-start(f32[1024,256]{1,0:T(8,128)} %shard_map.47), channel_id=1, source_target_pairs={{4,8},{5,9},{6,10},{7,11},{12,16},{13,17},{14,18},{15,19},{20,24},... | collective-permute-start | bytes 3145736 | tf_op jit(solution)/shard_map/ppermute | solution.py:291
  123.9 12.1 %collective-permute-start.17 = (f32[8,128]{1,0:T(8,128)S(1)}, f32[8,128]{1,0:T(8,128)S(1)}, u32[]{:S(2)}, u32[]{:S(2)}) collective-permute-start(f32[8,128]{1,0:T(8,128)S(1)} %slice.13), channel_id=1, source_target_pairs={{0,4},{1,5},{2,6},{3,7},{8,12},{9,13},{10,14},{11,15},{16,20},{17,... | collective-permute-start | bytes 12296 | tf_op jit(solution)/shard_map/ppermute | solution.py:291
  136.1 0.6 copy-start.4

commit v4 on v3

--- a/solution.py
+++ b/solution.py
@@ -66,8 +66,12 @@
     )(*[pltpu.with_memory_space_constraint(a, pltpu.HBM) for a in args])
 
 
-def only(on, index):
-    return lambda i: jnp.where(place()[1] == on, index(i), 0)
+def only(on, since, index):
+    def at(i):
+        k, core, _ = place()
+        return jnp.where((core == on) & (k >= since), index(i), 0)
+
+    return at
 
 
 def product_kernel(n_left, picks, width, on, since, *refs):
@@ -98,7 +102,7 @@
     rows, depth = left[0][0].shape[-2:]
     width = right[0][0].shape[-1]
     n, full = len(right), len(left) * depth
-    step = only(on, lambda i: i)
+    step = only(on, since, lambda i: i)
     return call_kernel(
         functools.partial(product_kernel, len(left), [p[1] for p in right], width, on, since),
         jax.ShapeDtypeStruct((n, rows, width), jnp.float32),
@@ -165,13 +169,13 @@
     tiles, n = rows // CHAIN_TILE, len(lefts)
     specs = []
     for m, left in enumerate(lefts):
-        specs += [spec(p, CHAIN_TILE, only(on, lambda i, m=m: jnp.clip(i - m * tiles, 0, tiles - 1))) for p in left]
+        specs += [spec(p, CHAIN_TILE, only(on, since, lambda i, m=m: jnp.clip(i - m * tiles, 0, tiles - 1))) for p in left]
     return call_kernel(
         functools.partial(chain_kernel, [len(left) for left in lefts], tiles, on, since, passes),
         jax.ShapeDtypeStruct((rows, width), jnp.float32),
         n * tiles,
         specs + [spec(right, rows, lambda i: 0)],
-        pl.BlockSpec((CHAIN_TILE, width), lambda i: (only(on, lambda i: jnp.maximum(i - (n - 1) * tiles, 0))(i), 0)),
+        pl.BlockSpec((CHAIN_TILE, width), lambda i: (only(on, since, lambda i: jnp.maximum(i - (n - 1) * tiles, 0))(i), 0)),
         [pltpu.VMEM((2, 3 * rows, width), jnp.bfloat16)],
         [p[0] for left in lefts for p in left] + [right[0]],
         6 * n * rows * rows * width,

time: 140 us -> 140 us (level)
  the two profiles are of different devices: /device:TPU:1 before, /device:TPU:255 now
where the time goes in v4:
time: 140 us; the launch traced here: 139 us
  Pallas kernels  51.9 us (37%)
  waiting for transfers between devices  39.9 us (28%)
  starting transfers between devices  38.6 us (28%)
  local copies, waits for them, and re-layouts  7.84 us (6%)
    pallas_call x8, Pallas kernels, call_kernel(): pl.pallas_call(kernel, out_shape=out_shape, grid=(grid,), in_specs=specs,...  51.9 us
    ppermute x18, waiting for transfers between devices, send(): return lax.ppermute(a, ('tm', 'panel'), pairs)  39.9 us
    ppermute x18, starting transfers between devices, send(): return lax.ppermute(a, ('tm', 'panel'), pairs)  38.6 us
    unnamed x16, local copies, waits for them, and re-layouts  4.58 us
  transfers between devices with their start and end apart: 18, of which 7 were waited for; matrix products, arithmetic and copies ran while one was open for 1% of the time, Pallas kernels for 34%

profile of v4, /device:TPU:255, one launch (start us, length us, event | category | flops | bytes accessed | tf_op | source)
XLA Modules:
  0.0 139.1 jit_solution(645769537068298719)
XLA Ops:
  0.6 1.3 slice_bitcast_fusion.1
  1.9 4.4 %collective-permute-start.1 = (f32[1024,256]{1,0:T(8,128)S(1)}, f32[1024,256]{1,0:T(8,128)S(1)}, u32[]{:S(2)}, u32[]{:S(2)}) collective-permute-start(f32[1024,256]{1,0:T(8,128)S(1)} %slice_bitcast_fusion.1), channel_id=1, source_target_pairs={{0,1},{1,2},{2,3},{3,0},{4,12},{5,13},{6,14},{7,15},{8,9},{9,10},{... | collective-permute-start | bytes 3145736 | tf_op jit(solution)/shard_map/ppermute | solution.py:295
  6.3 1.3 slice_bitcast_fusion
  7.6 0.7 collective-permute-start.3
  8.4 3.2 %collective-permute-start.5 = (f32[1024,256]{1,0:T(8,128)S(1)}, f32[1024,256]{1,0:T(8,128)}, u32[]{:S(2)}, u32[]{:S(2)}) collective-permute-start(f32[1024,256]{1,0:T(8,128)S(1)} %slice_bitcast_fusion), channel_id=1, source_target_pairs={{0,1},{1,2},{2,3},{3,0},{4,12},{5,13},{6,14},{7,15},{8,9},{9,10},{... | collective-permute-start | bytes 3145736 | tf_op jit(solution)/shard_map/ppermute | solution.py:295
  11.6 0.7 collective-permute-start
  12.3 5.7 %collective-permute-done.1.refs_3_.refs_0_ = f32[1024,256]{1,0:T(8,128)S(1)} collective-permute-done((f32[1024,256]{1,0:T(8,128)S(1)}, f32[1024,256]{1,0:T(8,128)S(1)}, u32[]{:S(2)}, u32[]{:S(2)}) %collective-permute-start.1) | collective-permute-done | bytes 1048608 | tf_op jit(solution)/shard_map/ppermute | solution.py:295
  18.1 0.7 collective-permute-start.2
  18.8 0.0 collective-permute-done.3.refs_5_
  18.8 1.6 %collective-permute-start.4 = (f32[1024,256]{1,0:T(8,128)S(1)}, f32[1024,256]{1,0:T(8,128)}, u32[]{:S(2)}, u32[]{:S(2)}) collective-permute-start(f32[1024,256]{1,0:T(8,128)S(1)} %collective-permute-done.3.refs_5_), channel_id=1, source_target_pairs={{0,3},{1,0},{2,1},{3,2},{8,11},{9,8},{10,9},{11,10},{16,19},{17,16... | collective-permute-start | bytes 3145736 | tf_op jit(solution)/shard_map/ppermute | solution.py:295
  20.5 8.9 %collective-permute-done.5.refs_7_.refs_0_.refs_3_ = f32[1024,256]{1,0:T(8,128)} collective-permute-done((f32[1024,256]{1,0:T(8,128)S(1)}, f32[1024,256]{1,0:T(8,128)}, u32[]{:S(2)}, u32[]{:S(2)}) %collective-permute-start.5) | collective-permute-done | bytes 1048608 | tf_op jit(solution)/shard_map/ppermute | solution.py:295
  29.3 0.0 collective-permute-done.refs_1_
  29.3 0.0 collective-permute-done.2.refs_2_
  29.3 1.0 copy-done.6
  30.3 1.0 copy-done.7
  31.3 2.2 %shard_map.41.whole = f32[4,1024,256]{2,1,0:T(8,128)} custom-call(f32[2,1024,256]{2,1,0:T(8,128)} %refs_4_.1, f32[1024,256]{1,0:T(8,128)} %copy-done.6, f32[1024,256]{1,0:T(8,128)} %copy-done.7, f32[1024,256]{1,0:T(8,128)} %copy-done.3, f32[2,1024,256]{2,1,0:T(8,128)} %refs_4_.1, f32[1024,256]{1,0:T(8,128)} %copy-done.5, ...), custom_call_target="tpu_custom_call" | custom-call | flops 6442450944 | bytes 12582912 | tf_op jit(solution)/shard_map/pallas_call | solution.py:57
  33.5 1.3 collective-permute-start.6
  34.8 2.1 %collective-permute-start.11 = (f32[1024,256]{1,0:T(8,128)}, f32[1024,256]{1,0:T(8,128)S(1)}, u32[]{:S(2)}, u32[]{:S(2)}) collective-permute-start(f32[1024,256]{1,0:T(8,128)} %collective-permute-done.5.refs_7_.refs_0_.refs_3_), channel_id=1, source_target_pairs={{12,13},{13,14},{14,15},{15,12},{20,21},{21,22},{22,23},{23,20},{2... | collective-permute-start | bytes 3145736 | tf_op jit(solution)/shard_map/ppermute | solution.py:295
  36.9 3.2 %collective-permute-start.10 = (f32[1024,256]{1,0:T(8,128)}, f32[1024,256]{1,0:T(8,128)S(1)}, u32[]{:S(2)}, u32[]{:S(2)}) collective-permute-start(f32[1024,256]{1,0:T(8,128)} %collective-permute-done.5.refs_7_.refs_0_.refs_3_), channel_id=1, source_target_pairs={{12,15},{13,12},{14,13},{15,14},{20,23},{21,20},{22,21},{23,22},{2... | collective-permute-start | bytes 3145736 | tf_op jit(solution)/shard_map/ppermute | solution.py:295
  40.1 2.5 %collective-permute-start.7 = (f32[1024,256]{1,0:T(8,128)}, f32[1024,256]{1,0:T(8,128)}, u32[]{:S(2)}, u32[]{:S(2)}) collective-permute-start(f32[1024,256]{1,0:T(8,128)} %copy-done.3), channel_id=1, source_target_pairs={{4,7},{5,4},{6,5},{7,6},{12,15},{13,12},{14,13},{15,14},{20,23},{2... | collective-permute-start | bytes 3145736 | tf_op jit(solution)/shard_map/ppermute | solution.py:295
  42.6 1.3 collective-permute-start.13
  43.9 8.4 %collective-permute-done.11.refs_3_.refs_6_ = f32[1024,256]{1,0:T(8,128)S(1)} collective-permute-done((f32[1024,256]{1,0:T(8,128)}, f32[1024,256]{1,0:T(8,128)S(1)}, u32[]{:S(2)}, u32[]{:S(2)}) %collective-permute-start.11) | collective-permute-done | bytes 1048608 | tf_op jit(solution)/shard_map/ppermute | solution.py:295
  52.3 1.1 copy-done
  53.4 3.3 %collective-permute-start.12 = (f32[1024,256]{1,0:T(8,128)S(1)}, f32[1024,256]{1,0:T(8,128)S(1)}, u32[]{:S(2)}, u32[]{:S(2)}) collective-permute-start(f32[1024,256]{1,0:T(8,128)S(1)} %collective-permute-done.11.refs_3_.refs_6_), channel_id=1, source_target_pairs={{12,13},{13,14},{14,15},{15,12},{20,21},{21,22},{22,23},{23,20},{2... | collective-permute-start | bytes 3145736 | tf_op jit(solution)/shard_map/ppermute | solution.py:295
  56.7 0.5 collective-permute-done.10.refs_1_.refs_4_
  57.2 1.9 %collective-permute-start.9 = (f32[1024,256]{1,0:T(8,128)}, f32[1024,256]{1,0:T(8,128)}, u32[]{:S(2)}, u32[]{:S(2)}) collective-permute-start(f32[1024,256]{1,0:T(8,128)} %copy-done.3), channel_id=1, source_target_pairs={{4,5},{5,6},{6,7},{7,4},{12,13},{13,14},{14,15},{15,12},{20,21},{2... | collective-permute-start | bytes 3145736 | tf_op jit(solution)/shard_map/ppermute | solution.py:295
  59.1 9.4 %collective-permute-done.7.refs_1_ = f32[1024,256]{1,0:T(8,128)} collective-permute-done((f32[1024,256]{1,0:T(8,128)}, f32[1024,256]{1,0:T(8,128)}, u32[]{:S(2)}, u32[]{:S(2)}) %collective-permute-start.7) | collective-permute-done | bytes 1048608 | tf_op jit(solution)/shard_map/ppermute | solution.py:295
  68.6 2.0 %collective-permute-start.8 = (f32[1024,256]{1,0:T(8,128)}, f32[1024,256]{1,0:T(8,128)}, u32[]{:S(2)}, u32[]{:S(2)}) collective-permute-start(f32[1024,256]{1,0:T(8,128)} %collective-permute-done.7.refs_1_), channel_id=1, source_target_pairs={{4,7},{5,4},{6,5},{7,6},{12,15},{13,12},{14,13},{15,14},{20,23},{2... | collective-permute-start | bytes 3145736 | tf_op jit(solution)/shard_map/ppermute | solution.py:295
  70.5 0.0 collective-permute-done.12.refs_2_.refs_5_
  70.6 1.0 copy-done.2
  71.5 5.0 %shard_map.42.refs_2_ = f32[1024,256]{1,0:T(8,128)} custom-call(f32[1024,256]{1,0:T(8,128)} %collective-permute-done.5.refs_7_.refs_0_.refs_3_, f32[1024,256]{1,0:T(8,128)} %copy-done.1, f32[1024,256]{1,0:T(8,128)} %copy-done.2, f32[1024,256]{1,0:T(8,128)} %copy-done, f32[4,1024,256]{2,1,0:T(8,128)} %collective-permute-done.6.refs_4_.refs_5_.refs_0_.refs_1_.refs_2_.refs_3_), custom_call_target="tpu_custom_call" | custom-call | flops 1610612736 | bytes 6291456 | tf_op jit(solution)/shard_map/pallas_call | solution.py:57
  76.6 5.0 %shard_map.43.refs_4_ = f32[2,1024,256]{2,1,0:T(8,128)} custom-call(f32[1024,256]{1,0:T(8,128)} %copy-done.3, f32[1024,256]{1,0:T(8,128)} %collective-permute-done.7.refs_1_, f32[1024,256]{1,0:T(8,128)} %shard_map.42.refs_2_, f32[1024,256]{1,0:T(8,128)} %collective-permute-done.5.refs_7_.refs_0_.refs_3_), custom_call_target="tpu_custom_call" | custom-call | flops 1610612736 | bytes 8388608 | tf_op jit(solution)/shard_map/pallas_call | solution.py:57
  81.6 0.0 collective-permute-done.9.refs_1_.refs_3_
  81.6 4.0 %collective-permute-done.8.refs_0_.refs_2_ = f32[1024,256]{1,0:T(8,128)} collective-permute-done((f32[1024,256]{1,0:T(8,128)}, f32[1024,256]{1,0:T(8,128)}, u32[]{:S(2)}, u32[]{:S(2)}) %collective-permute-start.8) | collective-permute-done | bytes 1048608 | tf_op jit(solution)/shard_map/ppermute | solution.py:295
  85.6 5.5 %shard_map.44 = (f32[1024,256]{1,0:T(8,128)}, f32[1024,256]{1,0:T(8,128)}) custom-call(f32[1024,256]{1,0:T(8,128)} %collective-permute-done.8.refs_0_.refs_2_, f32[1024,256]{1,0:T(8,128)} %collective-permute-done.9.refs_1_.refs_3_, f32[1024,256]{1,0:T(8,128)} %shard_map.42.refs_2_, f32[1024,256]{1,0:T(8,128)} %collective-permute-done.5.refs_7_.refs_0_.refs_3_, ...), custom_call_target="tpu_custom_call" | custom-call | flops 1610612736 | bytes 8388608 | tf_op jit(solution)/shard_map/pallas_call | solution.py:57
  91.1 3.0 %collective-permute-start.15 = (f32[1024,256]{1,0:T(8,128)}, f32[1024,256]{1,0:T(8,128)}, u32[]{:S(2)}, u32[]{:S(2)}) collective-permute-start(f32[1024,256]{1,0:T(8,128)} %get-tuple-element.7), channel_id=1, source_target_pairs={{12,4},{13,5},{14,6},{15,7},{20,12},{21,13},{22,14},{23,15},{28,20... | collective-permute-start | bytes 3145736 | tf_op jit(solution)/shard_map/ppermute | solution.py:295
  94.1 3.0 %collective-permute-start.14 = (f32[1024,256]{1,0:T(8,128)}, f32[1024,256]{1,0:T(8,128)}, u32[]{:S(2)}, u32[]{:S(2)}) collective-permute-start(f32[1024,256]{1,0:T(8,128)} %get-tuple-element.6.refs_4_), channel_id=1, source_target_pairs={{4,508},{5,509},{6,510},{7,511},{12,4},{13,5},{14,6},{15,7},{20,12... | collective-permute-start | bytes 3145736 | tf_op jit(solution)/shard_map/ppermute | solution.py:295
  97.1 10.3 %shard_map.45.refs_5_.refs_6_.refs_7_ = f32[3,1024,256]{2,1,0:T(8,128)} custom-call(f32[1024,256]{1,0:T(8,128)} %copy-done.3, f32[1024,256]{1,0:T(8,128)} %collective-permute-done.7.refs_1_, f32[1024,256]{1,0:T(8,128)} %collective-permute-done.8.refs_0_.refs_2_, f32[1024,256]{1,0:T(8,128)} %collective-permute-done.9.refs_1_.refs_3_, f32[1024,256]{1,0:T(8,128)} %copy-done.1, ...), custom_call_target="tpu_custom_call" | custom-call | flops 4831838208 | bytes 10485760 | tf_op jit(solution)/shard_map/pallas_call | solution.py:57
  107.4 2.9 %collective-permute-done.15.refs_8_ = f32[1024,256]{1,0:T(8,128)} collective-permute-done((f32[1024,256]{1,0:T(8,128)}, f32[1024,256]{1,0:T(8,128)}, u32[]{:S(2)}, u32[]{:S(2)}) %collective-permute-start.15) | collective-permute-done | bytes 1048608 | tf_op jit(solution)/shard_map/ppermute | solution.py:295
  110.3 8.5 %shard_map.47 = f32[1024,256]{1,0:T(8,128)} custom-call(f32[4,1024,256]{2,1,0:T(8,128)} %collective-permute-done.6.refs_4_.refs_5_.refs_0_.refs_1_.refs_2_.refs_3_, f32[4,1024,256]{2,1,0:T(8,128)} %collective-permute-done.6.refs_4_.refs_5_.refs_0_.refs_1_.refs_2_.refs_3_, ...), custom_call_target="tpu_custom_call" | custom-call | flops 3221225472 | bytes 10485760 | tf_op jit(solution)/shard_map/pallas_call | solution.py:57
  118.8 2.3 %collective-permute-start.16 = (f32[1024,256]{1,0:T(8,128)}, f32[1024,256]{1,0:T(8,128)}, u32[]{:S(2)}, u32[]{:S(2)}) collective-permute-start(f32[1024,256]{1,0:T(8,128)} %shard_map.47), channel_id=1, source_target_pairs={{4,8},{5,9},{6,10},{7,11},{12,16},{13,17},{14,18},{15,19},{20,24},... | collective-permute-start | bytes 3145736 | tf_op jit(solution)/shard_map/ppermute | solution.py:295
  121.1 0.7 slice.13
  121.8 1.5 %collective-permute-start.17 = (f32[8,128]{1,0:T(8,128)S(1)}, f32[8,128]{1,0:T(8,128)S(1)}, u32[]{:S(2)}, u32[]{:S(2)}) collective-permute-start(f32[8,128]{1,0:T(8,128)S(1)} %slice.13), channel_id=1, source_target_pairs={{0,4},{1,5},{2,6},{3,7},{8,12},{9,13},{10,14},{11,15},{16,20},{17,... | collective-permute-start | bytes 12296 | tf_op jit(solution)/shard_map/ppermute | solution.py:295
  123.3 0.0 collective-permute-done.14.refs_12_
  123.3 12.5 %shard_map.46.late = f32[1024,256]{1,0:T(8,128)} custom-call(f32[4,1024,256]{2,1,0:T(8,128)} %collective-permute-done.6.refs_4_.refs_5_.refs_0_.refs_1_.refs_2_.refs_3_, f32[4,1024,256]{2,1,0:T(8,128)} %collective-permute-done.6.refs_4_.refs_5_.refs_0_.refs_1_.refs_2_.refs_3_, ...), custom_call_target="tpu_custom_call" | custom-call | flops 4831838208 | bytes 14680064 | tf_op jit(solution)/shard_map/pallas_call | solution.py:57
  135.8 0.0 collective-permute-done.17.token
  135.8 0.6 copy-done.4
  136.4 2.7 %shard_map.48 = (f32[1024,256]{1,0:T(8,128)}, f32[1,256]{1,0:T(1,128)}) custom-call(f32[1024,256]{1,0:T(8,128)} %shard_map.46.late, f32[4,1024,256]{2,1,0:T(8,128)} %shard_map.41.whole, f32[1024,256]{1,0:T(8,128)} %collective-permute-done.16.early, f32[1,1024]{1,0:T(1,128)} %bitcast.6, f32[8,128]{1,0:T(8,128)} %copy-done.4), custom_call_target="tpu_custom_call" | custom-call | flops 1048576 | bytes 4194304 | tf_op jit(solution)/shard_map/pallas_call | solution.py:57
  (15 shorter events, 0.0 us)
Async XLA Ops:
  1.9 16.1 %collective-permute-start.1 = (f32[1024,256]{1,0:T(8,128)S(1)}, f32[1024,256]{1,0:T(8,128)S(1)}, u32[]{:S(2)}, u32[]{:S(2)}) collective-permute-start(f32[1024,256]{1,0:T(8,128)S(1)} %slice_bitcast_fusion.1), channel_id=1, source_target_pairs={{0,1},{1,2},{2,3},{3,0},{4,12},{5,13},{6,14},{7,15},{8,9},{9,10},{... | collective-permute-start | bytes 3145736 | tf_op jit(solution)/shard_map/ppermute | solution.py:295
  7.6 11.2 %collective-permute-start.3 = (f32[1024,256]{1,0:T(8,128)S(1)}, f32[1024,256]{1,0:T(8,128)S(1)}, u32[]{:S(2)}, u32[]{:S(2)}) collective-permute-start(f32[1024,256]{1,0:T(8,128)S(1)} %slice_bitcast_fusion), channel_id=1, source_target_pairs={{0,3},{1,0},{2,1},{3,2},{8,11},{9,8},{10,9},{11,10},{16,19},{17,16... | collective-permute-start | bytes 3145736 | tf_op jit(solution)/shard_map/ppermute | solution.py:295
  8.4 20.9 %collective-permute-start.5 = (f32[1024,256]{1,0:T(8,128)S(1)}, f32[1024,256]{1,0:T(8,128)}, u32[]{:S(2)}, u32[]{:S(2)}) collective-permute-start(f32[1024,256]{1,0:T(8,128)S(1)} %slice_bitcast_fusion), channel_id=1, source_target_pairs={{0,1},{1,2},{2,3},{3,0},{4,12},{5,13},{6,14},{7,15},{8,9},{9,10},{... | collective-permute-start | bytes 3145736 | tf_op jit(solution)/shard_map/ppermute | solution.py:295
  11.6 17.7 %collective-permute-start = (f32[1024,256]{1,0:T(8,128)S(1)}, f32[1024,256]{1,0:T(8,128)S(1)}, u32[]{:S(2)}, u32[]{:S(2)}) collective-permute-start(f32[1024,256]{1,0:T(8,128)S(1)} %slice_bitcast_fusion.1), channel_id=1, source_target_pairs={{0,3},{1,0},{2,1},{3,2},{8,11},{9,8},{10,9},{11,10},{16,19},{17,16... | collective-permute-start | bytes 3145736 | tf_op jit(solution)/shard_map/ppermute | solution.py:295
  18.1 11.2 %copy-start.3 = (f32[1024,256]{1,0:T(8,128)}, f32[1024,256]{1,0:T(8,128)S(1)}, u32[]{:S(2)}) copy-start(f32[1024,256]{1,0:T(8,128)S(1)} %collective-permute-done.1.refs_3_.refs_0_) | copy-start | bytes 3145732
  18.1 11.2 %collective-permute-start.2 = (f32[1024,256]{1,0:T(8,128)S(1)}, f32[1024,256]{1,0:T(8,128)S(1)}, u32[]{:S(2)}, u32[]{:S(2)}) collective-permute-start(f32[1024,256]{1,0:T(8,128)S(1)} %collective-permute-done.1.refs_3_.refs_0_), channel_id=1, source_target_pairs={{0,1},{1,2},{2,3},{3,0},{8,9},{9,10},{10,11},{11,8},{16,17},{17,18... | collective-permute-start | bytes 3145736 | tf_op jit(solution)/shard_map/ppermute | solution.py:295
  18.8 10.5 %copy-start.5 = (f32[1024,256]{1,0:T(8,128)}, f32[1024,256]{1,0:T(8,128)S(1)}, u32[]{:S(2)}) copy-start(f32[1024,256]{1,0:T(8,128)S(1)} %collective-permute-done.3.refs_5_) | copy-start | bytes 3145732
  18.8 12.5 %collective-permute-start.4 = (f32[1024,256]{1,0:T(8,128)S(1)}, f32[1024,256]{1,0:T(8,128)}, u32[]{:S(2)}, u32[]{:S(2)}) collective-permute-start(f32[1024,256]{1,0:T(8,128)S(1)} %collective-permute-done.3.refs_5_), channel_id=1, source_target_pairs={{0,3},{1,0},{2,1},{3,2},{8,11},{9,8},{10,9},{11,10},{16,19},{17,16... | collective-permute-start | bytes 3145736 | tf_op jit(solution)/shard_map/ppermute | solution.py:295
  29.3 1.0 copy-start.6
  30.3 1.0 copy-start.7
  33.5 38.0 %collective-permute-start.6 = (f32[4,1024,256]{2,1,0:T(8,128)}, f32[4,1024,256]{2,1,0:T(8,128)}, u32[]{:S(2)}, u32[]{:S(2)}) collective-permute-start(f32[4,1024,256]{2,1,0:T(8,128)} %shard_map.41.whole), channel_id=1, source_target_pairs={{0,4},{1,5},{2,6},{3,7},{8,12},{9,13},{10,14},{11,15},{16,20},{17,... | collective-permute-start | bytes 12582920 | tf_op jit(solution)/shard_map/ppermute | solution.py:295
  34.8 17.5 %collective-permute-start.11 = (f32[1024,256]{1,0:T(8,128)}, f32[1024,256]{1,0:T(8,128)S(1)}, u32[]{:S(2)}, u32[]{:S(2)}) collective-permute-start(f32[1024,256]{1,0:T(8,128)} %collective-permute-done.5.refs_7_.refs_0_.refs_3_), channel_id=1, source_target_pairs={{12,13},{13,14},{14,15},{15,12},{20,21},{21,22},{22,23},{23,20},{2... | collective-permute-start | bytes 3145736 | tf_op jit(solution)/shard_map/ppermute | solution.py:295
  36.9 20.3 %collective-permute-start.10 = (f32[1024,256]{1,0:T(8,128)}, f32[1024,256]{1,0:T(8,128)S(1)}, u32[]{:S(2)}, u32[]{:S(2)}) collective-permute-start(f32[1024,256]{1,0:T(8,128)} %collective-permute-done.5.refs_7_.refs_0_.refs_3_), channel_id=1, source_target_pairs={{12,15},{13,12},{14,13},{15,14},{20,23},{21,20},{22,21},{23,22},{2... | collective-permute-start | bytes 3145736 | tf_op jit(solution)/shard_map/ppermute | solution.py:295
  40.1 28.4 %collective-permute-start.7 = (f32[1024,256]{1,0:T(8,128)}, f32[1024,256]{1,0:T(8,128)}, u32[]{:S(2)}, u32[]{:S(2)}) collective-permute-start(f32[1024,256]{1,0:T(8,128)} %copy-done.3), channel_id=1, source_target_pairs={{4,7},{5,4},{6,5},{7,6},{12,15},{13,12},{14,13},{15,14},{20,23},{2... | collective-permute-start | bytes 3145736 | tf_op jit(solution)/shard_map/ppermute | solution.py:295
  42.6 80.7 %collective-permute-start.13 = (f32[4,1024,256]{2,1,0:T(8,128)}, f32[4,1024,256]{2,1,0:T(8,128)}, u32[]{:S(2)}, u32[]{:S(2)}) collective-permute-start(f32[4,1024,256]{2,1,0:T(8,128)} %shard_map.41.whole), channel_id=1, source_target_pairs={{0,12},{1,13},{2,14},{3,15},{8,20},{9,21},{10,22},{11,23},{16,28},... | collective-permute-start | bytes 12582920 | tf_op jit(solution)/shard_map/ppermute | solution.py:295
  52.3 1.1 copy-start
  53.4 17.1 %collective-permute-start.12 = (f32[1024,256]{1,0:T(8,128)S(1)}, f32[1024,256]{1,0:T(8,128)S(1)}, u32[]{:S(2)}, u32[]{:S(2)}) collective-permute-start(f32[1024,256]{1,0:T(8,128)S(1)} %collective-permute-done.11.refs_3_.refs_6_), channel_id=1, source_target_pairs={{12,13},{13,14},{14,15},{15,12},{20,21},{21,22},{22,23},{23,20},{2... | collective-permute-start | bytes 3145736 | tf_op jit(solution)/shard_map/ppermute | solution.py:295
  57.2 13.3 %copy-start.1 = (f32[1024,256]{1,0:T(8,128)}, f32[1024,256]{1,0:T(8,128)S(1)}, u32[]{:S(2)}) copy-start(f32[1024,256]{1,0:T(8,128)S(1)} %collective-permute-done.10.refs_1_.refs_4_) | copy-start | bytes 3145732
  57.2 24.4 %collective-permute-start.9 = (f32[1024,256]{1,0:T(8,128)}, f32[1024,256]{1,0:T(8,128)}, u32[]{:S(2)}, u32[]{:S(2)}) collective-permute-start(f32[1024,256]{1,0:T(8,128)} %copy-done.3), channel_id=1, source_target_pairs={{4,5},{5,6},{6,7},{7,4},{12,13},{13,14},{14,15},{15,12},{20,21},{2... | collective-permute-start | bytes 3145736 | tf_op jit(solution)/shard_map/ppermute | solution.py:295
  68.6 17.1 %collective-permute-start.8 = (f32[1024,256]{1,0:T(8,128)}, f32[1024,256]{1,0:T(8,128)}, u32[]{:S(2)}, u32[]{:S(2)}) collective-permute-start(f32[1024,256]{1,0:T(8,128)} %collective-permute-done.7.refs_1_), channel_id=1, source_target_pairs={{4,7},{5,4},{6,5},{7,6},{12,15},{13,12},{14,13},{15,14},{20,23},{2... | collective-permute-start | bytes 3145736 | tf_op jit(solution)/shard_map/ppermute | solution.py:295
  70.5 1.0 copy-start.2
  91.1 19.2 %collective-permute-start.15 = (f32[1024,256]{1,0:T(8,128)}, f32[1024,256]{1,0:T(8,128)}, u32[]{:S(2)}, u32[]{:S(2)}) collective-permute-start(f32[1024,256]{1,0:T(8,128)} %get-tuple-element.7), channel_id=1, source_target_pairs={{12,4},{13,5},{14,6},{15,7},{20,12},{21,13},{22,14},{23,15},{28,20... | collective-permute-start | bytes 3145736 | tf_op jit(solution)/shard_map/ppermute | solution.py:295
  94.1 29.2 %collective-permute-start.14 = (f32[1024,256]{1,0:T(8,128)}, f32[1024,256]{1,0:T(8,128)}, u32[]{:S(2)}, u32[]{:S(2)}) collective-permute-start(f32[1024,256]{1,0:T(8,128)} %get-tuple-element.6.refs_4_), channel_id=1, source_target_pairs={{4,508},{5,509},{6,510},{7,511},{12,4},{13,5},{14,6},{15,7},{20,12... | collective-permute-start | bytes 3145736 | tf_op jit(solution)/shard_map/ppermute | solution.py:295
  118.8 17.0 %collective-permute-start.16 = (f32[1024,256]{1,0:T(8,128)}, f32[1024,256]{1,0:T(8,128)}, u32[]{:S(2)}, u32[]{:S(2)}) collective-permute-start(f32[1024,256]{1,0:T(8,128)} %shard_map.47), channel_id=1, source_target_pairs={{4,8},{5,9},{6,10},{7,11},{12,16},{13,17},{14,18},{15,19},{20,24},... | collective-permute-start | bytes 3145736 | tf_op jit(solution)/shard_map/ppermute | solution.py:295
  121.8 14.0 %collective-permute-start.17 = (f32[8,128]{1,0:T(8,128)S(1)}, f32[8,128]{1,0:T(8,128)S(1)}, u32[]{:S(2)}, u32[]{:S(2)}) collective-permute-start(f32[8,128]{1,0:T(8,128)S(1)} %slice.13), channel_id=1, source_target_pairs={{0,4},{1,5},{2,6},{3,7},{8,12},{9,13},{10,14},{11,15},{16,20},{17,... | collective-permute-start | bytes 12296 | tf_op jit(solution)/shard_map/ppermute | solution.py:295
  135.8 0.6 copy-start.4

commit v5 on v4

--- a/solution.py
+++ b/solution.py
@@ -98,7 +98,7 @@
             out[j] = total[:, j * width : (j + 1) * width]
 
 
-def product(left, right, on, since=0):
+def product(left, right, on, since=0, tile=TILE):
     rows, depth = left[0][0].shape[-2:]
     width = right[0][0].shape[-1]
     n, full = len(right), len(left) * depth
@@ -106,9 +106,9 @@
     return call_kernel(
         functools.partial(product_kernel, len(left), [p[1] for p in right], width, on, since),
         jax.ShapeDtypeStruct((n, rows, width), jnp.float32),
-        rows // TILE,
-        [spec(p, TILE, step) for p in left] + [pl.BlockSpec(memory_space=pl.ANY)] * n,
-        pl.BlockSpec((n, TILE, width), lambda i: (0, step(i), 0)),
+        rows // tile,
+        [spec(p, tile, step) for p in left] + [pl.BlockSpec(memory_space=pl.ANY)] * n,
+        pl.BlockSpec((n, tile, width), lambda i: (0, step(i), 0)),
         [
             pltpu.VMEM((n, rows, width), jnp.float32),
             pltpu.VMEM((3 * full, n * width), jnp.bfloat16),
@@ -332,7 +332,7 @@
     there = send(step, None, (-1, 1, 0))
     own = ahead
     ahead = send(ahead, None, (-1, 1, 0), wrap=True)
-    rest = product(left, right[1:], 1, since=1)
+    rest = product(left, right[1:], 1, since=1, tile=CHAIN_TILE)
     odd = [(own, None)] + [(rest, j) for j in range(n_x - 1)]
     step = chain([even_here, odd], (there, None), 1, (False, True))
     early = send(step, None, (1, 0, 0))

time: 140 us -> 140 us (level)
  no operation moved by 1% of the time
where the time goes in v5:
time: 140 us; the launch traced here: 139 us
  Pallas kernels  51.8 us (37%)
  waiting for transfers between devices  39.7 us (28%)
  starting transfers between devices  38.6 us (28%)
  local copies, waits for them, and re-layouts  7.84 us (6%)
    pallas_call x8, Pallas kernels, call_kernel(): pl.pallas_call(kernel, out_shape=out_shape, grid=(grid,), in_specs=specs,...  51.8 us
    ppermute x18, waiting for transfers between devices, send(): return lax.ppermute(a, ('tm', 'panel'), pairs)  39.7 us
    ppermute x18, starting transfers between devices, send(): return lax.ppermute(a, ('tm', 'panel'), pairs)  38.6 us
    unnamed x16, local copies, waits for them, and re-layouts  4.58 us
  transfers between devices with their start and end apart: 18, of which 7 were waited for; matrix products, arithmetic and copies ran while one was open for 1% of the time, Pallas kernels for 34%

profile of v5, /device:TPU:255, one launch (start us, length us, event | category | flops | bytes accessed | tf_op | source)
XLA Modules:
  0.0 138.9 jit_solution(16483402631348793353)
XLA Ops:
  0.6 1.3 slice_bitcast_fusion.1
  1.9 4.4 %collective-permute-start.1 = (f32[1024,256]{1,0:T(8,128)S(1)}, f32[1024,256]{1,0:T(8,128)S(1)}, u32[]{:S(2)}, u32[]{:S(2)}) collective-permute-start(f32[1024,256]{1,0:T(8,128)S(1)} %slice_bitcast_fusion.1), channel_id=1, source_target_pairs={{0,1},{1,2},{2,3},{3,0},{4,12},{5,13},{6,14},{7,15},{8,9},{9,10},{... | collective-permute-start | bytes 3145736 | tf_op jit(solution)/shard_map/ppermute | solution.py:295
  6.3 1.3 slice_bitcast_fusion
  7.6 0.7 collective-permute-start.3
  8.4 3.2 %collective-permute-start.5 = (f32[1024,256]{1,0:T(8,128)S(1)}, f32[1024,256]{1,0:T(8,128)}, u32[]{:S(2)}, u32[]{:S(2)}) collective-permute-start(f32[1024,256]{1,0:T(8,128)S(1)} %slice_bitcast_fusion), channel_id=1, source_target_pairs={{0,1},{1,2},{2,3},{3,0},{4,12},{5,13},{6,14},{7,15},{8,9},{9,10},{... | collective-permute-start | bytes 3145736 | tf_op jit(solution)/shard_map/ppermute | solution.py:295
  11.6 0.7 collective-permute-start
  12.3 5.7 %collective-permute-done.1.refs_3_.refs_0_ = f32[1024,256]{1,0:T(8,128)S(1)} collective-permute-done((f32[1024,256]{1,0:T(8,128)S(1)}, f32[1024,256]{1,0:T(8,128)S(1)}, u32[]{:S(2)}, u32[]{:S(2)}) %collective-permute-start.1) | collective-permute-done | bytes 1048608 | tf_op jit(solution)/shard_map/ppermute | solution.py:295
  18.1 0.7 collective-permute-start.2
  18.8 0.0 collective-permute-done.3.refs_5_
  18.8 1.6 %collective-permute-start.4 = (f32[1024,256]{1,0:T(8,128)S(1)}, f32[1024,256]{1,0:T(8,128)}, u32[]{:S(2)}, u32[]{:S(2)}) collective-permute-start(f32[1024,256]{1,0:T(8,128)S(1)} %collective-permute-done.3.refs_5_), channel_id=1, source_target_pairs={{0,3},{1,0},{2,1},{3,2},{8,11},{9,8},{10,9},{11,10},{16,19},{17,16... | collective-permute-start | bytes 3145736 | tf_op jit(solution)/shard_map/ppermute | solution.py:295
  20.5 8.9 %collective-permute-done.5.refs_7_.refs_0_.refs_3_ = f32[1024,256]{1,0:T(8,128)} collective-permute-done((f32[1024,256]{1,0:T(8,128)S(1)}, f32[1024,256]{1,0:T(8,128)}, u32[]{:S(2)}, u32[]{:S(2)}) %collective-permute-start.5) | collective-permute-done | bytes 1048608 | tf_op jit(solution)/shard_map/ppermute | solution.py:295
  29.3 0.0 collective-permute-done.refs_1_
  29.3 0.0 collective-permute-done.2.refs_2_
  29.3 1.0 copy-done.6
  30.3 1.0 copy-done.7
  31.3 0.0 collective-permute-done.4.refs_6_
  31.3 2.2 %shard_map.41.whole = f32[4,1024,256]{2,1,0:T(8,128)} custom-call(f32[2,1024,256]{2,1,0:T(8,128)} %refs_4_.1, f32[1024,256]{1,0:T(8,128)} %copy-done.6, f32[1024,256]{1,0:T(8,128)} %copy-done.7, f32[1024,256]{1,0:T(8,128)} %copy-done.3, f32[2,1024,256]{2,1,0:T(8,128)} %refs_4_.1, f32[1024,256]{1,0:T(8,128)} %copy-done.5, ...), custom_call_target="tpu_custom_call" | custom-call | flops 6442450944 | bytes 12582912 | tf_op jit(solution)/shard_map/pallas_call | solution.py:57
  33.5 1.3 collective-permute-start.6
  34.8 2.1 %collective-permute-start.11 = (f32[1024,256]{1,0:T(8,128)}, f32[1024,256]{1,0:T(8,128)S(1)}, u32[]{:S(2)}, u32[]{:S(2)}) collective-permute-start(f32[1024,256]{1,0:T(8,128)} %collective-permute-done.5.refs_7_.refs_0_.refs_3_), channel_id=1, source_target_pairs={{12,13},{13,14},{14,15},{15,12},{20,21},{21,22},{22,23},{23,20},{2... | collective-permute-start | bytes 3145736 | tf_op jit(solution)/shard_map/ppermute | solution.py:295
  36.9 3.2 %collective-permute-start.10 = (f32[1024,256]{1,0:T(8,128)}, f32[1024,256]{1,0:T(8,128)S(1)}, u32[]{:S(2)}, u32[]{:S(2)}) collective-permute-start(f32[1024,256]{1,0:T(8,128)} %collective-permute-done.5.refs_7_.refs_0_.refs_3_), channel_id=1, source_target_pairs={{12,15},{13,12},{14,13},{15,14},{20,23},{21,20},{22,21},{23,22},{2... | collective-permute-start | bytes 3145736 | tf_op jit(solution)/shard_map/ppermute | solution.py:295
  40.1 2.5 %collective-permute-start.7 = (f32[1024,256]{1,0:T(8,128)}, f32[1024,256]{1,0:T(8,128)}, u32[]{:S(2)}, u32[]{:S(2)}) collective-permute-start(f32[1024,256]{1,0:T(8,128)} %copy-done.3), channel_id=1, source_target_pairs={{4,7},{5,4},{6,5},{7,6},{12,15},{13,12},{14,13},{15,14},{20,23},{2... | collective-permute-start | bytes 3145736 | tf_op jit(solution)/shard_map/ppermute | solution.py:295
  42.6 1.3 collective-permute-start.13
  43.9 8.4 %collective-permute-done.11.refs_3_.refs_6_ = f32[1024,256]{1,0:T(8,128)S(1)} collective-permute-done((f32[1024,256]{1,0:T(8,128)}, f32[1024,256]{1,0:T(8,128)S(1)}, u32[]{:S(2)}, u32[]{:S(2)}) %collective-permute-start.11) | collective-permute-done | bytes 1048608 | tf_op jit(solution)/shard_map/ppermute | solution.py:295
  52.3 1.1 copy-done
  53.4 3.3 %collective-permute-start.12 = (f32[1024,256]{1,0:T(8,128)S(1)}, f32[1024,256]{1,0:T(8,128)S(1)}, u32[]{:S(2)}, u32[]{:S(2)}) collective-permute-start(f32[1024,256]{1,0:T(8,128)S(1)} %collective-permute-done.11.refs_3_.refs_6_), channel_id=1, source_target_pairs={{12,13},{13,14},{14,15},{15,12},{20,21},{21,22},{22,23},{23,20},{2... | collective-permute-start | bytes 3145736 | tf_op jit(solution)/shard_map/ppermute | solution.py:295
  56.7 0.5 collective-permute-done.10.refs_1_.refs_4_
  57.2 1.9 %collective-permute-start.9 = (f32[1024,256]{1,0:T(8,128)}, f32[1024,256]{1,0:T(8,128)}, u32[]{:S(2)}, u32[]{:S(2)}) collective-permute-start(f32[1024,256]{1,0:T(8,128)} %copy-done.3), channel_id=1, source_target_pairs={{4,5},{5,6},{6,7},{7,4},{12,13},{13,14},{14,15},{15,12},{20,21},{2... | collective-permute-start | bytes 3145736 | tf_op jit(solution)/shard_map/ppermute | solution.py:295
  59.1 9.4 %collective-permute-done.7.refs_1_ = f32[1024,256]{1,0:T(8,128)} collective-permute-done((f32[1024,256]{1,0:T(8,128)}, f32[1024,256]{1,0:T(8,128)}, u32[]{:S(2)}, u32[]{:S(2)}) %collective-permute-start.7) | collective-permute-done | bytes 1048608 | tf_op jit(solution)/shard_map/ppermute | solution.py:295
  68.6 2.0 %collective-permute-start.8 = (f32[1024,256]{1,0:T(8,128)}, f32[1024,256]{1,0:T(8,128)}, u32[]{:S(2)}, u32[]{:S(2)}) collective-permute-start(f32[1024,256]{1,0:T(8,128)} %collective-permute-done.7.refs_1_), channel_id=1, source_target_pairs={{4,7},{5,4},{6,5},{7,6},{12,15},{13,12},{14,13},{15,14},{20,23},{2... | collective-permute-start | bytes 3145736 | tf_op jit(solution)/shard_map/ppermute | solution.py:295
  70.5 0.0 collective-permute-done.12.refs_2_.refs_5_
  70.6 1.0 copy-done.2
  71.5 5.0 %shard_map.42.refs_2_ = f32[1024,256]{1,0:T(8,128)} custom-call(f32[1024,256]{1,0:T(8,128)} %collective-permute-done.5.refs_7_.refs_0_.refs_3_, f32[1024,256]{1,0:T(8,128)} %copy-done.1, f32[1024,256]{1,0:T(8,128)} %copy-done.2, f32[1024,256]{1,0:T(8,128)} %copy-done, f32[4,1024,256]{2,1,0:T(8,128)} %collective-permute-done.6.refs_4_.refs_5_.refs_0_.refs_1_.refs_2_.refs_3_), custom_call_target="tpu_custom_call" | custom-call | flops 1610612736 | bytes 6291456 | tf_op jit(solution)/shard_map/pallas_call | solution.py:57
  76.6 5.0 %shard_map.43.refs_4_ = f32[2,1024,256]{2,1,0:T(8,128)} custom-call(f32[1024,256]{1,0:T(8,128)} %copy-done.3, f32[1024,256]{1,0:T(8,128)} %collective-permute-done.7.refs_1_, f32[1024,256]{1,0:T(8,128)} %shard_map.42.refs_2_, f32[1024,256]{1,0:T(8,128)} %collective-permute-done.5.refs_7_.refs_0_.refs_3_), custom_call_target="tpu_custom_call" | custom-call | flops 1610612736 | bytes 8388608 | tf_op jit(solution)/shard_map/pallas_call | solution.py:57
  81.6 0.0 collective-permute-done.9.refs_1_.refs_3_
  81.6 4.0 %collective-permute-done.8.refs_0_.refs_2_ = f32[1024,256]{1,0:T(8,128)} collective-permute-done((f32[1024,256]{1,0:T(8,128)}, f32[1024,256]{1,0:T(8,128)}, u32[]{:S(2)}, u32[]{:S(2)}) %collective-permute-start.8) | collective-permute-done | bytes 1048608 | tf_op jit(solution)/shard_map/ppermute | solution.py:295
  85.6 5.5 %shard_map.44 = (f32[1024,256]{1,0:T(8,128)}, f32[1024,256]{1,0:T(8,128)}) custom-call(f32[1024,256]{1,0:T(8,128)} %collective-permute-done.8.refs_0_.refs_2_, f32[1024,256]{1,0:T(8,128)} %collective-permute-done.9.refs_1_.refs_3_, f32[1024,256]{1,0:T(8,128)} %shard_map.42.refs_2_, f32[1024,256]{1,0:T(8,128)} %collective-permute-done.5.refs_7_.refs_0_.refs_3_, ...), custom_call_target="tpu_custom_call" | custom-call | flops 1610612736 | bytes 8388608 | tf_op jit(solution)/shard_map/pallas_call | solution.py:57
  91.1 3.0 %collective-permute-start.15 = (f32[1024,256]{1,0:T(8,128)}, f32[1024,256]{1,0:T(8,128)}, u32[]{:S(2)}, u32[]{:S(2)}) collective-permute-start(f32[1024,256]{1,0:T(8,128)} %get-tuple-element.7), channel_id=1, source_target_pairs={{12,4},{13,5},{14,6},{15,7},{20,12},{21,13},{22,14},{23,15},{28,20... | collective-permute-start | bytes 3145736 | tf_op jit(solution)/shard_map/ppermute | solution.py:295
  94.1 3.2 %collective-permute-start.14 = (f32[1024,256]{1,0:T(8,128)}, f32[1024,256]{1,0:T(8,128)}, u32[]{:S(2)}, u32[]{:S(2)}) collective-permute-start(f32[1024,256]{1,0:T(8,128)} %get-tuple-element.6.refs_4_), channel_id=1, source_target_pairs={{4,508},{5,509},{6,510},{7,511},{12,4},{13,5},{14,6},{15,7},{20,12... | collective-permute-start | bytes 3145736 | tf_op jit(solution)/shard_map/ppermute | solution.py:295
  97.3 10.3 %shard_map.45.refs_5_.refs_6_.refs_7_ = f32[3,1024,256]{2,1,0:T(8,128)} custom-call(f32[1024,256]{1,0:T(8,128)} %copy-done.3, f32[1024,256]{1,0:T(8,128)} %collective-permute-done.7.refs_1_, f32[1024,256]{1,0:T(8,128)} %collective-permute-done.8.refs_0_.refs_2_, f32[1024,256]{1,0:T(8,128)} %collective-permute-done.9.refs_1_.refs_3_, f32[1024,256]{1,0:T(8,128)} %copy-done.1, ...), custom_call_target="tpu_custom_call" | custom-call | flops 4831838208 | bytes 10485760 | tf_op jit(solution)/shard_map/pallas_call | solution.py:57
  107.6 2.7 %collective-permute-done.15.refs_8_ = f32[1024,256]{1,0:T(8,128)} collective-permute-done((f32[1024,256]{1,0:T(8,128)}, f32[1024,256]{1,0:T(8,128)}, u32[]{:S(2)}, u32[]{:S(2)}) %collective-permute-start.15) | collective-permute-done | bytes 1048608 | tf_op jit(solution)/shard_map/ppermute | solution.py:295
  110.3 8.5 %shard_map.47 = f32[1024,256]{1,0:T(8,128)} custom-call(f32[4,1024,256]{2,1,0:T(8,128)} %collective-permute-done.6.refs_4_.refs_5_.refs_0_.refs_1_.refs_2_.refs_3_, f32[4,1024,256]{2,1,0:T(8,128)} %collective-permute-done.6.refs_4_.refs_5_.refs_0_.refs_1_.refs_2_.refs_3_, ...), custom_call_target="tpu_custom_call" | custom-call | flops 3221225472 | bytes 10485760 | tf_op jit(solution)/shard_map/pallas_call | solution.py:57
  118.8 2.3 %collective-permute-start.16 = (f32[1024,256]{1,0:T(8,128)}, f32[1024,256]{1,0:T(8,128)}, u32[]{:S(2)}, u32[]{:S(2)}) collective-permute-start(f32[1024,256]{1,0:T(8,128)} %shard_map.47), channel_id=1, source_target_pairs={{4,8},{5,9},{6,10},{7,11},{12,16},{13,17},{14,18},{15,19},{20,24},... | collective-permute-start | bytes 3145736 | tf_op jit(solution)/shard_map/ppermute | solution.py:295
  121.1 0.7 slice.13
  121.8 1.3 collective-permute-start.17
  123.1 12.5 %shard_map.46.late = f32[1024,256]{1,0:T(8,128)} custom-call(f32[4,1024,256]{2,1,0:T(8,128)} %collective-permute-done.6.refs_4_.refs_5_.refs_0_.refs_1_.refs_2_.refs_3_, f32[4,1024,256]{2,1,0:T(8,128)} %collective-permute-done.6.refs_4_.refs_5_.refs_0_.refs_1_.refs_2_.refs_3_, ...), custom_call_target="tpu_custom_call" | custom-call | flops 4831838208 | bytes 14680064 | tf_op jit(solution)/shard_map/pallas_call | solution.py:57
  135.6 0.0 collective-permute-done.17.token
  135.6 0.6 copy-done.4
  136.2 2.7 %shard_map.48 = (f32[1024,256]{1,0:T(8,128)}, f32[1,256]{1,0:T(1,128)}) custom-call(f32[1024,256]{1,0:T(8,128)} %shard_map.46.late, f32[4,1024,256]{2,1,0:T(8,128)} %shard_map.41.whole, f32[1024,256]{1,0:T(8,128)} %collective-permute-done.16.early, f32[1,1024]{1,0:T(1,128)} %bitcast.6, f32[8,128]{1,0:T(8,128)} %copy-done.4), custom_call_target="tpu_custom_call" | custom-call | flops 1048576 | bytes 4194304 | tf_op jit(solution)/shard_map/pallas_call | solution.py:57
  (15 shorter events, 0.0 us)
Async XLA Ops:
  1.9 16.1 %collective-permute-start.1 = (f32[1024,256]{1,0:T(8,128)S(1)}, f32[1024,256]{1,0:T(8,128)S(1)}, u32[]{:S(2)}, u32[]{:S(2)}) collective-permute-start(f32[1024,256]{1,0:T(8,128)S(1)} %slice_bitcast_fusion.1), channel_id=1, source_target_pairs={{0,1},{1,2},{2,3},{3,0},{4,12},{5,13},{6,14},{7,15},{8,9},{9,10},{... | collective-permute-start | bytes 3145736 | tf_op jit(solution)/shard_map/ppermute | solution.py:295
  7.6 11.2 %collective-permute-start.3 = (f32[1024,256]{1,0:T(8,128)S(1)}, f32[1024,256]{1,0:T(8,128)S(1)}, u32[]{:S(2)}, u32[]{:S(2)}) collective-permute-start(f32[1024,256]{1,0:T(8,128)S(1)} %slice_bitcast_fusion), channel_id=1, source_target_pairs={{0,3},{1,0},{2,1},{3,2},{8,11},{9,8},{10,9},{11,10},{16,19},{17,16... | collective-permute-start | bytes 3145736 | tf_op jit(solution)/shard_map/ppermute | solution.py:295
  8.4 20.9 %collective-permute-start.5 = (f32[1024,256]{1,0:T(8,128)S(1)}, f32[1024,256]{1,0:T(8,128)}, u32[]{:S(2)}, u32[]{:S(2)}) collective-permute-start(f32[1024,256]{1,0:T(8,128)S(1)} %slice_bitcast_fusion), channel_id=1, source_target_pairs={{0,1},{1,2},{2,3},{3,0},{4,12},{5,13},{6,14},{7,15},{8,9},{9,10},{... | collective-permute-start | bytes 3145736 | tf_op jit(solution)/shard_map/ppermute | solution.py:295
  11.6 17.7 %collective-permute-start = (f32[1024,256]{1,0:T(8,128)S(1)}, f32[1024,256]{1,0:T(8,128)S(1)}, u32[]{:S(2)}, u32[]{:S(2)}) collective-permute-start(f32[1024,256]{1,0:T(8,128)S(1)} %slice_bitcast_fusion.1), channel_id=1, source_target_pairs={{0,3},{1,0},{2,1},{3,2},{8,11},{9,8},{10,9},{11,10},{16,19},{17,16... | collective-permute-start | bytes 3145736 | tf_op jit(solution)/shard_map/ppermute | solution.py:295
  18.1 11.2 %copy-start.3 = (f32[1024,256]{1,0:T(8,128)}, f32[1024,256]{1,0:T(8,128)S(1)}, u32[]{:S(2)}) copy-start(f32[1024,256]{1,0:T(8,128)S(1)} %collective-permute-done.1.refs_3_.refs_0_) | copy-start | bytes 3145732
  18.1 11.2 %collective-permute-start.2 = (f32[1024,256]{1,0:T(8,128)S(1)}, f32[1024,256]{1,0:T(8,128)S(1)}, u32[]{:S(2)}, u32[]{:S(2)}) collective-permute-start(f32[1024,256]{1,0:T(8,128)S(1)} %collective-permute-done.1.refs_3_.refs_0_), channel_id=1, source_target_pairs={{0,1},{1,2},{2,3},{3,0},{8,9},{9,10},{10,11},{11,8},{16,17},{17,18... | collective-permute-start | bytes 3145736 | tf_op jit(solution)/shard_map/ppermute | solution.py:295
  18.8 10.5 %copy-start.5 = (f32[1024,256]{1,0:T(8,128)}, f32[1024,256]{1,0:T(8,128)S(1)}, u32[]{:S(2)}) copy-start(f32[1024,256]{1,0:T(8,128)S(1)} %collective-permute-done.3.refs_5_) | copy-start | bytes 3145732
  18.8 12.5 %collective-permute-start.4 = (f32[1024,256]{1,0:T(8,128)S(1)}, f32[1024,256]{1,0:T(8,128)}, u32[]{:S(2)}, u32[]{:S(2)}) collective-permute-start(f32[1024,256]{1,0:T(8,128)S(1)} %collective-permute-done.3.refs_5_), channel_id=1, source_target_pairs={{0,3},{1,0},{2,1},{3,2},{8,11},{9,8},{10,9},{11,10},{16,19},{17,16... | collective-permute-start | bytes 3145736 | tf_op jit(solution)/shard_map/ppermute | solution.py:295
  29.3 1.0 copy-start.6
  30.3 1.0 copy-start.7
  33.5 38.0 %collective-permute-start.6 = (f32[4,1024,256]{2,1,0:T(8,128)}, f32[4,1024,256]{2,1,0:T(8,128)}, u32[]{:S(2)}, u32[]{:S(2)}) collective-permute-start(f32[4,1024,256]{2,1,0:T(8,128)} %shard_map.41.whole), channel_id=1, source_target_pairs={{0,4},{1,5},{2,6},{3,7},{8,12},{9,13},{10,14},{11,15},{16,20},{17,... | collective-permute-start | bytes 12582920 | tf_op jit(solution)/shard_map/ppermute | solution.py:295
  34.8 17.5 %collective-permute-start.11 = (f32[1024,256]{1,0:T(8,128)}, f32[1024,256]{1,0:T(8,128)S(1)}, u32[]{:S(2)}, u32[]{:S(2)}) collective-permute-start(f32[1024,256]{1,0:T(8,128)} %collective-permute-done.5.refs_7_.refs_0_.refs_3_), channel_id=1, source_target_pairs={{12,13},{13,14},{14,15},{15,12},{20,21},{21,22},{22,23},{23,20},{2... | collective-permute-start | bytes 3145736 | tf_op jit(solution)/shard_map/ppermute | solution.py:295
  36.9 20.3 %collective-permute-start.10 = (f32[1024,256]{1,0:T(8,128)}, f32[1024,256]{1,0:T(8,128)S(1)}, u32[]{:S(2)}, u32[]{:S(2)}) collective-permute-start(f32[1024,256]{1,0:T(8,128)} %collective-permute-done.5.refs_7_.refs_0_.refs_3_), channel_id=1, source_target_pairs={{12,15},{13,12},{14,13},{15,14},{20,23},{21,20},{22,21},{23,22},{2... | collective-permute-start | bytes 3145736 | tf_op jit(solution)/shard_map/ppermute | solution.py:295
  40.1 28.4 %collective-permute-start.7 = (f32[1024,256]{1,0:T(8,128)}, f32[1024,256]{1,0:T(8,128)}, u32[]{:S(2)}, u32[]{:S(2)}) collective-permute-start(f32[1024,256]{1,0:T(8,128)} %copy-done.3), channel_id=1, source_target_pairs={{4,7},{5,4},{6,5},{7,6},{12,15},{13,12},{14,13},{15,14},{20,23},{2... | collective-permute-start | bytes 3145736 | tf_op jit(solution)/shard_map/ppermute | solution.py:295
  42.6 80.5 %collective-permute-start.13 = (f32[4,1024,256]{2,1,0:T(8,128)}, f32[4,1024,256]{2,1,0:T(8,128)}, u32[]{:S(2)}, u32[]{:S(2)}) collective-permute-start(f32[4,1024,256]{2,1,0:T(8,128)} %shard_map.41.whole), channel_id=1, source_target_pairs={{0,12},{1,13},{2,14},{3,15},{8,20},{9,21},{10,22},{11,23},{16,28},... | collective-permute-start | bytes 12582920 | tf_op jit(solution)/shard_map/ppermute | solution.py:295
  52.3 1.1 copy-start
  53.4 17.1 %collective-permute-start.12 = (f32[1024,256]{1,0:T(8,128)S(1)}, f32[1024,256]{1,0:T(8,128)S(1)}, u32[]{:S(2)}, u32[]{:S(2)}) collective-permute-start(f32[1024,256]{1,0:T(8,128)S(1)} %collective-permute-done.11.refs_3_.refs_6_), channel_id=1, source_target_pairs={{12,13},{13,14},{14,15},{15,12},{20,21},{21,22},{22,23},{23,20},{2... | collective-permute-start | bytes 3145736 | tf_op jit(solution)/shard_map/ppermute | solution.py:295
  57.2 13.3 %copy-start.1 = (f32[1024,256]{1,0:T(8,128)}, f32[1024,256]{1,0:T(8,128)S(1)}, u32[]{:S(2)}) copy-start(f32[1024,256]{1,0:T(8,128)S(1)} %collective-permute-done.10.refs_1_.refs_4_) | copy-start | bytes 3145732
  57.2 24.4 %collective-permute-start.9 = (f32[1024,256]{1,0:T(8,128)}, f32[1024,256]{1,0:T(8,128)}, u32[]{:S(2)}, u32[]{:S(2)}) collective-permute-start(f32[1024,256]{1,0:T(8,128)} %copy-done.3), channel_id=1, source_target_pairs={{4,5},{5,6},{6,7},{7,4},{12,13},{13,14},{14,15},{15,12},{20,21},{2... | collective-permute-start | bytes 3145736 | tf_op jit(solution)/shard_map/ppermute | solution.py:295
  68.6 17.1 %collective-permute-start.8 = (f32[1024,256]{1,0:T(8,128)}, f32[1024,256]{1,0:T(8,128)}, u32[]{:S(2)}, u32[]{:S(2)}) collective-permute-start(f32[1024,256]{1,0:T(8,128)} %collective-permute-done.7.refs_1_), channel_id=1, source_target_pairs={{4,7},{5,4},{6,5},{7,6},{12,15},{13,12},{14,13},{15,14},{20,23},{2... | collective-permute-start | bytes 3145736 | tf_op jit(solution)/shard_map/ppermute | solution.py:295
  70.5 1.0 copy-start.2
  91.1 19.2 %collective-permute-start.15 = (f32[1024,256]{1,0:T(8,128)}, f32[1024,256]{1,0:T(8,128)}, u32[]{:S(2)}, u32[]{:S(2)}) collective-permute-start(f32[1024,256]{1,0:T(8,128)} %get-tuple-element.7), channel_id=1, source_target_pairs={{12,4},{13,5},{14,6},{15,7},{20,12},{21,13},{22,14},{23,15},{28,20... | collective-permute-start | bytes 3145736 | tf_op jit(solution)/shard_map/ppermute | solution.py:295
  94.1 29.0 %collective-permute-start.14 = (f32[1024,256]{1,0:T(8,128)}, f32[1024,256]{1,0:T(8,128)}, u32[]{:S(2)}, u32[]{:S(2)}) collective-permute-start(f32[1024,256]{1,0:T(8,128)} %get-tuple-element.6.refs_4_), channel_id=1, source_target_pairs={{4,508},{5,509},{6,510},{7,511},{12,4},{13,5},{14,6},{15,7},{20,12... | collective-permute-start | bytes 3145736 | tf_op jit(solution)/shard_map/ppermute | solution.py:295
  118.8 16.8 %collective-permute-start.16 = (f32[1024,256]{1,0:T(8,128)}, f32[1024,256]{1,0:T(8,128)}, u32[]{:S(2)}, u32[]{:S(2)}) collective-permute-start(f32[1024,256]{1,0:T(8,128)} %shard_map.47), channel_id=1, source_target_pairs={{4,8},{5,9},{6,10},{7,11},{12,16},{13,17},{14,18},{15,19},{20,24},... | collective-permute-start | bytes 3145736 | tf_op jit(solution)/shard_map/ppermute | solution.py:295
  121.8 13.8 %collective-permute-start.17 = (f32[8,128]{1,0:T(8,128)S(1)}, f32[8,128]{1,0:T(8,128)S(1)}, u32[]{:S(2)}, u32[]{:S(2)}) collective-permute-start(f32[8,128]{1,0:T(8,128)S(1)} %slice.13), channel_id=1, source_target_pairs={{0,4},{1,5},{2,6},{3,7},{8,12},{9,13},{10,14},{11,15},{16,20},{17,... | collective-permute-start | bytes 12296 | tf_op jit(solution)/shard_map/ppermute | solution.py:295
  135.6 0.6 copy-start.4
